TPU v7x, 128 devices: a whole 4x4x4 slice. The times are simulated.
128 devices in a mesh: member: 8 (over z, x_hi), lon: 16 (over y, x_lo, core).
Axes of the slice: x: 4 (x_hi: 2, x_lo: 2; x = x_hi * 2 + x_lo), y: 4, z: 4, core: 2. Of those that a mesh axis runs over, the one named last changes fastest.
Arguments:
- latent: bfloat16 [16, 4, 720, 641], P('member', None, 'lon'), may hold values from -6 to 6
- member_seeds: int32 [16], P('member'), may hold values from 0 to 63
- member_table: bfloat16 [64, 641], replicated, may hold values from -6 to 6
- row_bands: int32 [4], replicated, may hold values from 0 to 15
- disco_basis: bfloat16 [16, 4, 7, 7], replicated, may hold values from -0.8984375 to 0.8984375
- w_disco: bfloat16 [2564, 641], replicated, may hold values from -0.125 to 0.125
- w_expand: bfloat16 [641, 1282], replicated, may hold values from -0.25 to 0.25
- w_reduce: bfloat16 [1282, 641], replicated, may hold values from -0.15625 to 0.15625
- w_decode: bfloat16 [641, 288], replicated, may hold values from -0.25 to 0.25
- target: bfloat16 [4, 720, 288], P(None, 'lon'), may hold values from -12 to 12
Outputs:
- latent_grad: bfloat16 [16, 4, 720, 641], P('member', None, 'lon')
- grad_disco: bfloat16 [2564, 641], replicated
- grad_expand: bfloat16 [641, 1282], replicated
- grad_reduce: bfloat16 [1282, 641], replicated
- grad_decode: bfloat16 [641, 288], replicated
All inputs are finite; a program needn't handle non-finite values.
Results may differ from a plain program's by a relative error of at most 0.025.
Values may be sent and summed in bfloat16 or wider, within the bound.
A program may use at most 128 MiB of HBM per device.

v0:
```python
import functools
import math

import jax
import jax.numpy as jnp
from jax import lax
from jax.experimental import pallas as pl
from jax.experimental.pallas import tpu as pltpu
from jax.sharding import PartitionSpec as P

MESH = pl.DeviceIdType.MESH
f32 = jnp.float32
bf16 = jnp.bfloat16

CH = 641
HID = 1282
OUTC = 288
WIDE = 2564
ROWS = 384
HALF = 192
TILES = 1920
PART = 320
AXES = (("x", "y", "z"), ("y", "z", "x"), ("z", "x", "y"))
OFF_DISCO, OFF_EXPAND, OFF_REDUCE, OFF_DECODE, OFF_TAIL = 0, 805, 1215, 1620, 1743
U_DISCO, U_EXPAND, U_REDUCE, U_DECODE = 161, 41, 81, 41


def place():
    member, lon = lax.axis_index("member"), lax.axis_index("lon")
    return {
        "x": (member % 2) * 2 + (lon // 2) % 2,
        "y": lon // 4,
        "z": member // 2,
        "c": lon % 2,
    }


def device(at):
    return (at["z"] * 2 + at["x"] // 2, at["y"] * 4 + (at["x"] % 2) * 2 + at["c"])


def moved(at, axis, step):
    there = dict(at)
    size = 2 if axis == "c" else 4
    there[axis] = lax.rem(at[axis] + step + size, size)
    return there


def iota(shape, dim):
    return lax.broadcasted_iota(jnp.int32, shape, dim)


def dot(a, b):
    return jnp.dot(a, b, preferred_element_type=f32)


def dot_nt(a, b):
    return lax.dot_general(a, b, (((1,), (1,)), ((), ())), preferred_element_type=f32)


def flat_tiles(value):
    return value.astype(bf16).reshape(value.shape[0] // 16, 16, 128)


class Copies:
    def __init__(self, send_sems, recv_sems):
        self.send_sems, self.recv_sems, self.count = send_sems, recv_sems, 0
        self.started = []

    def send(self, src, dst, to):
        copy = pltpu.make_async_remote_copy(
            src_ref=src,
            dst_ref=dst,
            send_sem=self.send_sems.at[self.count],
            recv_sem=self.recv_sems.at[self.count],
            device_id=to,
            device_id_type=MESH,
        )
        self.count += 1
        copy.start()
        self.started.append(copy)
        return copy

    def finish(self):
        for copy in self.started:
            copy.wait_send()


def pair_slopes(fv, og, tgt, me_h, lanes, rows):
    lo, width = lanes
    values = [fv[j, rows, lo : lo + width] for j in range(16)]
    sums = [None] * 16

    def slope(d):
        return d * lax.rsqrt(d * d + 0.25)

    for i in range(16):
        for j in range(i + 1, 16):
            s = slope(values[i] - values[j])
            sums[i] = s if sums[i] is None else sums[i] + s
            sums[j] = -s if sums[j] is None else sums[j] - s
    goal = tgt[:, lo : lo + width]
    keep = me_h
    for i in range(16):
        value = slope(values[i] - goal) - sums[i] * (1.0 / 15.0)
        og[i, rows, lo : lo + width] = jnp.where(keep, value, 0.0)


def step_kernel(
    latent,
    seeds,
    table,
    bands,
    basis,
    wd_any,
    we_any,
    wr_any,
    wo_any,
    target,
    lg,
    flat,
    wd,
    we,
    wr,
    wo,
    tk,
    tt,
    wide,
    hs,
    spread,
    spread_t,
    hid,
    hid_t,
    gp,
    act,
    act_t,
    mix,
    mix_t,
    halo_s,
    halo_r,
    fs,
    fr,
    fv,
    og,
    gs,
    gr,
    tp,
    fg,
    mg,
    pg,
    hg,
    sgs,
    ob,
    back_r,
    grads,
    r0,
    r1,
    r2,
    r3,
    send_sems,
    recv_sems,
    load_sems,
):
    at = place()
    me = lax.axis_index("member")
    lon = lax.axis_index("lon")
    left = (me, lax.rem(lon + 15, 16))
    right = (me, lax.rem(lon + 1, 16))
    core = at["c"]
    copies = Copies(send_sems, recv_sems)

    loads = []
    for i, (src, dst) in enumerate(((wd_any, wd), (we_any, we), (wr_any, wr), (wo_any, wo))):
        load = pltpu.make_async_copy(src, dst, load_sems.at[i])
        load.start()
        loads.append(load)

    sibling = device(moved(at, "c", 1))
    barrier = pltpu.get_barrier_semaphore()
    greet = [sibling, left, right]
    greet += [device(moved(at, axis, d)) for axis in "xyz" for d in (1, 2, 3)]
    greet += [(lax.rem(me + d, 8), lon) for d in range(1, 8)]
    for peer in greet:
        pl.semaphore_signal(barrier, inc=1, device_id=peer, device_id_type=MESH)

    wide[...] = jnp.zeros_like(wide)
    hs[...] = jnp.zeros_like(hs)
    for ref in (hid, mix, mg, hg):
        ref[:, 640:768] = jnp.zeros((ROWS, 128), bf16)
    for ref in (act, pg):
        ref[:, 1280:1408] = jnp.zeros((ROWS, 128), bf16)
    fg[:, 256:384] = jnp.zeros((ROWS, 128), bf16)
    for m in range(2):
        pick = jnp.where(iota((8, 64), 1) == seeds[m], 1.0, 0.0).astype(bf16)
        offset = dot(pick, table[...])[0:1]
        for s in range(4):
            value = (latent[m, s].astype(f32) + offset).astype(bf16)
            wide[m, s * 64 : s * 64 + 45, 0:CH] = value
            hs[m * HALF + s * 48 : m * HALF + s * 48 + 45, 0:CH] = value

    row = iota((16, 256), 0)
    col = iota((16, 256), 1)
    third = lax.shift_right_logical(row * 11, 5)
    spot = third * 64 + (row - third * 3)
    first_pick = jnp.where((row < 12) & (col == spot), 1.0, 0.0).astype(bf16)
    last_pick = jnp.where((row < 12) & (col == spot + 42), 1.0, 0.0).astype(bf16)
    for m in range(2):
        halo_s[0, m] = dot(first_pick, wide[m]).astype(bf16)
        halo_s[1, m] = dot(last_pick, wide[m]).astype(bf16)

    pl.semaphore_wait(barrier, len(greet))
    from_right = copies.send(halo_s.at[0], halo_r.at[0], left)
    from_left = copies.send(halo_s.at[1], halo_r.at[1], right)

    keep_rows = iota((48, 256), 0) < 45
    for r in range(4):
        taps = basis[bands[r]].astype(f32)
        lines = None
        for s in range(4):
            a = s - r + 3
            some = jnp.concatenate([taps[k, a : a + 1, :] for k in range(4)], axis=0)
            some = jnp.concatenate([some, jnp.zeros((4, 249), f32)], axis=1)
            some = pltpu.roll(some, (s * 64 - 3) % 256, 1)
            lines = some if lines is None else lines + some
        for k in range(4):
            line = lines[k : k + 1]
            band = pltpu.roll(jnp.broadcast_to(line, (48, 256)), 0, 1, stride=1, stride_axis=0)
            tk[k, r * 48 : r * 48 + 48, :] = jnp.where(keep_rows, band, 0.0).astype(bf16)
    for k in range(4):
        tt[:, k * HALF : k * HALF + HALF] = tk[k].T
    tp[...] = jnp.zeros_like(tp)
    for r in range(4):
        tp[r, 0:45, :] = target[r].astype(f32)

    prow = iota((256, 16), 0)
    pcol = iota((256, 16), 1)
    third = lax.shift_right_logical(pcol * 11, 5)
    spot = third * 64 + (pcol - third * 3)
    put_right = jnp.where((pcol < 12) & (prow == spot + 45), 1.0, 0.0).astype(bf16)
    put_left = jnp.where((pcol < 12) & (prow == ((spot + 253) & 255)), 1.0, 0.0).astype(bf16)
    from_right.wait_recv()
    from_left.wait_recv()
    for m in range(2):
        halo = dot(put_right, halo_r[0, m]) + dot(put_left, halo_r[1, m])
        wide[m] = (wide[m].astype(f32) + halo).astype(bf16)

    for m in range(2):
        carry = None
        rows = slice(m * HALF, m * HALF + HALF)
        for k in range(4):
            value = dot(tk[k], wide[m])
            if k:
                value = pltpu.roll(value, k, 1)
            head = value[:, 0:128] if carry is None else value[:, 0:128] + carry
            spread[rows, 640 * k : 640 * k + 128] = head.astype(bf16)
            spread[rows, 640 * k + 128 : 640 * k + 640] = value[:, 128:640].astype(bf16)
            carry = value[:, 640:768]
        spread[rows, 2560:2688] = carry.astype(bf16)

    for load in loads:
        load.wait()
    conv = dot(spread[:, 0:WIDE], wd[...])
    hid[:, 0:CH] = (hs[:, 0:CH].astype(f32) + conv).astype(bf16)
    pre = dot(hid[:, 0:CH], we[...])
    inner = math.sqrt(2.0 / math.pi)
    square = pre * pre
    t = jnp.tanh(inner * (pre + 0.044715 * (square * pre)))
    act[:, 0:HID] = (0.5 * pre * (1.0 + t)).astype(bf16)
    gp[...] = 0.5 * (1.0 + t) + (0.5 * inner) * pre * (1.0 - t * t) * (
        1.0 + (3.0 * 0.044715) * square
    )
    mix[:, 0:CH] = (hid[:, 0:CH].astype(f32) + dot(act[:, 0:HID], wr[...])).astype(bf16)
    fields = dot(mix[:, 0:CH], wo[...])
    for p in range(8):
        block = jnp.concatenate(
            [fields[24 * p : 24 * p + 24], fields[HALF + 24 * p : HALF + 24 * p + 24]], axis=0
        )
        fs[p] = block.astype(bf16)
    there = []
    for d in range(1, 8):
        peer = lax.rem(me + d, 8)
        there.append(copies.send(fs.at[peer], fr.at[me], (peer, lon)))
    fr[me] = fs[me]

    spread_t[...] = spread[...].T
    hid_t[...] = hid[...].T
    act_t[...] = act[...].T
    mix_t[...] = mix[...].T

    for copy in there:
        copy.wait_recv()
    for p in range(8):
        block = fr[p].astype(f32)
        fv[2 * p] = block[0:24]
        fv[2 * p + 1] = block[24:48]
    slab, side = me // 2, lax.rem(me, 2)

    def slopes(i, carry):
        start = pl.multiple_of(i * 8, 8)
        rows = pl.ds(start, 8)
        goal = tp[slab, pl.ds(pl.multiple_of(side * 24 + start, 8), 8), :]
        for lanes in ((0, 128), (128, 128), (256, 32)):
            keep = iota((8, lanes[1]), 0) + (side * 24 + start) < 45
            pair_slopes(fv, og, goal, keep, lanes, rows)
        return carry

    lax.fori_loop(0, 3, slopes, 0)
    for p in range(8):
        gs[p] = jnp.concatenate([og[2 * p], og[2 * p + 1]], axis=0).astype(bf16)
    back = []
    for d in range(1, 8):
        peer = lax.rem(me + d, 8)
        back.append(copies.send(gs.at[peer], gr.at[me], (peer, lon)))
    gr[me] = gs[me]
    for copy in back:
        copy.wait_recv()
    blocks = [gr[p].astype(f32) for p in range(8)]
    fg[:, 0:OUTC] = jnp.concatenate(
        [b[0:24] for b in blocks] + [b[24:48] for b in blocks], axis=0
    ).astype(bf16)

    mixed_grad = dot_nt(fg[:, 0:OUTC], wo[...])
    mg[:, 0:CH] = mixed_grad.astype(bf16)
    pg[:, 0:HID] = (dot_nt(mg[:, 0:CH], wr[...]) * gp[...]).astype(bf16)
    hidden_grad = mg[:, 0:CH].astype(f32) + dot_nt(pg[:, 0:HID], we[...])
    hg[:, 0:CH] = hidden_grad.astype(bf16)

    def decode_part():
        value = dot(mix_t[0:656], fg[...])
        for j in range(3):
            grads[pl.ds(OFF_DECODE + j * U_DECODE, U_DECODE)] = flat_tiles(
                value[:, 128 * j : 128 * j + 128]
            )

    decode_part()
    grads[OFF_TAIL : OFF_TAIL + 177] = jnp.zeros((177, 16, 128), bf16)
    for c in range(3):
        value = dot(act_t[c * 432 : c * 432 + 432], mg[...])
        for j in range(5):
            grads[pl.ds(OFF_REDUCE + j * U_REDUCE + c * 27, 27)] = flat_tiles(
                value[:, 128 * j : 128 * j + 128]
            )
        grads[pl.ds(OFF_TAIL + c * 27, 27)] = flat_tiles(pltpu.roll(value[:, 640:768], 1, 1))
    value = dot(hid_t[0:656], pg[...])
    for j in range(10):
        grads[pl.ds(OFF_EXPAND + j * U_EXPAND, U_EXPAND)] = flat_tiles(
            value[:, 128 * j : 128 * j + 128]
        )
    tail = flat_tiles(pltpu.roll(value[:, 1280:1408], 2, 1))
    grads[pl.ds(OFF_TAIL, U_EXPAND)] = grads[pl.ds(OFF_TAIL, U_EXPAND)] + tail

    def disco_part(c, carry):
        value = dot(spread_t[pl.ds(pl.multiple_of(c * 368, 16), 368)], hg[...])
        for j in range(5):
            grads[pl.ds(OFF_DISCO + j * U_DISCO + c * 23, 23)] = flat_tiles(
                value[:, 128 * j : 128 * j + 128]
            )
        tail = flat_tiles(value[:, 640:768])
        spot = pl.ds(OFF_TAIL + c * 23, 23)
        grads[spot] = grads[spot] + tail
        return carry

    lax.fori_loop(0, 7, disco_part, 0)

    other = 1 - core
    waits = [
        copies.send(
            grads.at[pl.ds(other * 960 + p * PART, PART)], r0.at[pl.ds(p * PART, PART)], sibling
        )
        for p in range(3)
    ]

    for m in range(2):
        rows = slice(m * HALF, m * HALF + HALF)
        value = dot_nt(hg[rows, 0:CH], wd[...]).astype(bf16).astype(f32)
        value = jnp.concatenate([value, jnp.zeros((HALF, 124), f32)], axis=1)
        for k in range(4):
            piece = value[:, 640 * k : 640 * k + 768]
            if k:
                piece = pltpu.roll(piece, 768 - k, 1)
            sgs[k * HALF : k * HALF + HALF, :] = piece[:, 0:CH].astype(bf16)
        out = dot(tt[...], sgs[...])
        for s in range(4):
            ob[0, m, s] = out[((s + 3) % 4) * 64 + 56 : ((s + 3) % 4) * 64 + 64]
            ob[1, m, s] = out[s * 64 + 40 : s * 64 + 48]
            base = m * HALF + s * 48
            total = hg[base : base + 48, 0:CH].astype(f32) + out[s * 64 : s * 64 + 48]
            gp[base : base + 48, 0:CH] = total
    to_left = copies.send(ob.at[0], back_r.at[0], left)
    to_right = copies.send(ob.at[1], back_r.at[1], right)

    def add_tiles(dst, dst_at, parts, count, scale=None):
        step = 20 if count >= 20 else count

        def body(i, carry):
            total = None
            for ref, start in parts:
                piece = ref[pl.ds(start + i * step, step)].astype(f32)
                total = piece if total is None else total + piece
            if scale is not None:
                total = total * scale
            dst[pl.ds(dst_at + i * step, step)] = total.astype(bf16)
            return carry

        lax.fori_loop(0, count // step, body, 0)

    mine = [core * 960 + p * PART for p in range(3)]
    stage_a = []
    for p in range(3):
        waits[p].wait_recv()
        add_tiles(grads, mine[p], [(grads, mine[p]), (r0, p * PART)], PART)
        axis = AXES[p][0]
        for d in (1, 3, 2):
            there_at = moved(at, axis, d)
            stage_a.append(
                copies.send(
                    grads.at[pl.ds(mine[p] + there_at[axis] * 80, 80)],
                    r1.at[pl.ds((p * 3 + d - 1) * 80, 80)],
                    device(there_at),
                )
            )
    to_left.wait_recv()
    to_right.wait_recv()
    lane8 = iota((8, CH), 0)
    for m in range(2):
        for s in range(4):
            base = m * HALF + s * 48
            high = pltpu.roll(back_r[0, m, s], 5, 0)
            low = pltpu.roll(back_r[1, m, s], 3, 0)
            high = jnp.where((lane8 >= 2) & (lane8 < 5), high, 0.0)
            low = jnp.where(lane8 < 3, low, 0.0)
            gp[base : base + 8, 0:CH] = gp[base : base + 8, 0:CH] + low
            gp[base + 40 : base + 48, 0:CH] = gp[base + 40 : base + 48, 0:CH] + high
            lg[m, s] = gp[base : base + 48, 0:CH][0:45].astype(bf16)

    mine_a = [mine[p] + at[AXES[p][0]] * 80 for p in range(3)]
    mine_b = [mine_a[p] + at[AXES[p][1]] * 20 for p in range(3)]
    mine_c = [mine_b[p] + at[AXES[p][2]] * 5 for p in range(3)]
    stage_b = []
    for p in range(3):
        for copy in stage_a[3 * p : 3 * p + 3]:
            copy.wait_recv()
        add_tiles(
            grads,
            mine_a[p],
            [(grads, mine_a[p])] + [(r1, (p * 3 + d) * 80) for d in range(3)],
            80,
        )
        axis = AXES[p][1]
        for d in (1, 3, 2):
            there_at = moved(at, axis, d)
            stage_b.append(
                copies.send(
                    grads.at[pl.ds(mine_a[p] + there_at[axis] * 20, 20)],
                    r2.at[pl.ds((p * 3 + d - 1) * 20, 20)],
                    device(there_at),
                )
            )
    stage_c = []
    for p in range(3):
        for copy in stage_b[3 * p : 3 * p + 3]:
            copy.wait_recv()
        add_tiles(
            grads,
            mine_b[p],
            [(grads, mine_b[p])] + [(r2, (p * 3 + d) * 20) for d in range(3)],
            20,
        )
        axis = AXES[p][2]
        for d in (1, 3, 2):
            there_at = moved(at, axis, d)
            stage_c.append(
                copies.send(
                    grads.at[pl.ds(mine_b[p] + there_at[axis] * 5, 5)],
                    r3.at[pl.ds((p * 3 + d - 1) * 5, 5)],
                    device(there_at),
                )
            )
    factor = 1.0 / math.sqrt(46080.0)

    def spread_out(p, axis, start, count):
        region = flat.at[pl.ds(start, count)]
        return [
            copies.send(region, region, device(moved(at, axis, d))) for d in (1, 3, 2)
        ]

    gather_c = []
    for p in range(3):
        for copy in stage_c[3 * p : 3 * p + 3]:
            copy.wait_recv()
        add_tiles(
            flat,
            mine_c[p],
            [(grads, mine_c[p])] + [(r3, (p * 3 + d) * 5) for d in range(3)],
            5,
            factor,
        )
        gather_c.append(spread_out(p, AXES[p][2], mine_c[p], 5))
    gather_b = []
    for p in range(3):
        for copy in gather_c[p]:
            copy.wait_recv()
        gather_b.append(spread_out(p, AXES[p][1], mine_b[p], 20))
    gather_a = []
    for p in range(3):
        for copy in gather_b[p]:
            copy.wait_recv()
        gather_a.append(spread_out(p, AXES[p][0], mine_a[p], 80))
    last = []
    for p in range(3):
        region = flat.at[pl.ds(mine_a[p], 80)]
        last.append(copies.send(region, region, sibling))
    for p in range(3):
        axis = AXES[p][0]
        for d, copy in zip((1, 3, 2), gather_a[p]):
            copy.wait_recv()
            came = lax.rem(at[axis] + 4 - d, 4)
            region = flat.at[pl.ds(mine[p] + came * 80, 80)]
            last.append(copies.send(region, region, sibling))
    for copy in last:
        copy.wait_recv()
    copies.finish()


def unpack_kernel(flat, disco, expand, reduce, decode):
    def column(start, units):
        return flat[start : start + units].reshape(units * 16, 128)

    tail = column(OFF_TAIL, U_DISCO)
    for j in range(5):
        disco[:, 128 * j : 128 * j + 128] = column(OFF_DISCO + j * U_DISCO, U_DISCO)[0:WIDE]
        reduce[:, 128 * j : 128 * j + 128] = column(OFF_REDUCE + j * U_REDUCE, U_REDUCE)[0:HID]
    disco[:, 640:CH] = tail[0:WIDE, 0:1]
    wide_tail = tail.astype(f32)
    reduce[:, 640:CH] = pltpu.roll(wide_tail[0:1296], 127, 1)[0:HID, 0:1].astype(bf16)
    for j in range(10):
        expand[:, 128 * j : 128 * j + 128] = column(OFF_EXPAND + j * U_EXPAND, U_EXPAND)[0:CH]
    expand[:, 1280:HID] = pltpu.roll(wide_tail[0:656], 126, 1)[0:CH, 0:2].astype(bf16)
    for j in range(3):
        width = min(128, OUTC - 128 * j)
        piece = column(OFF_DECODE + j * U_DECODE, U_DECODE)[0:CH]
        decode[:, 128 * j : 128 * j + width] = piece[:, 0:width]


def per_device(
    latent,
    member_seeds,
    member_table,
    row_bands,
    disco_basis,
    w_disco,
    w_expand,
    w_reduce,
    w_decode,
    target,
):
    vm = pl.BlockSpec(memory_space=pltpu.VMEM)
    sm = pl.BlockSpec(memory_space=pltpu.SMEM)
    anywhere = pl.BlockSpec(memory_space=pl.ANY)
    V = pltpu.VMEM
    copies = 110
    scratch = [
        V((WIDE, CH), bf16),
        V((CH, HID), bf16),
        V((HID, CH), bf16),
        V((CH, OUTC), bf16),
        V((4, HALF, 256), bf16),
        V((256, 768), bf16),
        V((2, 256, 768), bf16),
        V((ROWS, 768), bf16),
        V((ROWS, 2688), bf16),
        V((2688, ROWS), bf16),
        V((ROWS, 768), bf16),
        V((768, ROWS), bf16),
        V((ROWS, HID), f32),
        V((ROWS, 1408), bf16),
        V((1408, ROWS), bf16),
        V((ROWS, 768), bf16),
        V((768, ROWS), bf16),
        V((2, 2, 16, 768), bf16),
        V((2, 2, 16, 768), bf16),
        V((8, 48, OUTC), bf16),
        V((8, 48, OUTC), bf16),
        V((16, 24, OUTC), f32),
        V((16, 24, OUTC), f32),
        V((8, 48, OUTC), bf16),
        V((8, 48, OUTC), bf16),
        V((4, 48, OUTC), f32),
        V((ROWS, 384), bf16),
        V((ROWS, 768), bf16),
        V((ROWS, 1408), bf16),
        V((ROWS, 768), bf16),
        V((768, CH), bf16),
        V((2, 2, 4, 8, CH), f32),
        V((2, 2, 4, 8, CH), f32),
        V((TILES, 16, 128), bf16),
        V((960, 16, 128), bf16),
        V((720, 16, 128), bf16),
        V((180, 16, 128), bf16),
        V((45, 16, 128), bf16),
        pltpu.SemaphoreType.DMA((copies,)),
        pltpu.SemaphoreType.DMA((copies,)),
        pltpu.SemaphoreType.DMA((4,)),
    ]
    lg, flat = pl.pallas_call(
        step_kernel,
        out_shape=(
            jax.ShapeDtypeStruct(latent.shape, bf16),
            jax.ShapeDtypeStruct((TILES, 16, 128), bf16),
        ),
        in_specs=[vm, sm, vm, sm, vm, anywhere, anywhere, anywhere, anywhere, vm],
        out_specs=(vm, vm),
        scratch_shapes=scratch,
        compiler_params=pltpu.CompilerParams(
            collective_id=0, has_side_effects=True, vmem_limit_bytes=66_000_000
        ),
        name="step",
    )(
        latent,
        member_seeds,
        member_table,
        row_bands,
        disco_basis,
        w_disco,
        w_expand,
        w_reduce,
        w_decode,
        target,
    )
    outs = pl.pallas_call(
        unpack_kernel,
        out_shape=(
            jax.ShapeDtypeStruct((WIDE, CH), bf16),
            jax.ShapeDtypeStruct((CH, HID), bf16),
            jax.ShapeDtypeStruct((HID, CH), bf16),
            jax.ShapeDtypeStruct((CH, OUTC), bf16),
        ),
        in_specs=[vm],
        out_specs=(vm, vm, vm, vm),
        compiler_params=pltpu.CompilerParams(vmem_limit_bytes=40_000_000),
        name="unpack",
    )(flat)
    return (lg,) + tuple(outs)


def solution(mesh):
    placed = (
        P("member", None, "lon", None),
        P("member"),
        P(),
        P(),
        P(),
        P(),
        P(),
        P(),
        P(),
        P(None, "lon", None),
    )
    return jax.shard_map(
        per_device,
        mesh=mesh,
        in_specs=placed,
        out_specs=(P("member", None, "lon", None), P(), P(), P(), P()),
        check_vma=False,
    )
```

profile of v0, /device:TPU:1, one launch (start us, length us, event | category | flops | bytes accessed | tf_op | source)
XLA Modules:
  0.0 145.4 jit_solution(14519299819237682715)
XLA Ops:
  0.6 1.8 %copy.16.basis = bf16[16,4,7,7]{3,2,1,0:T(8,128)(2,1)} copy(bf16[16,4,7,7]{0,1,3,2:T(4,128)(2,1)} %param.14) | data formatting | bytes 12544 | tf_op args[4]
  2.4 1.6 %copy.20.target = bf16[4,45,288]{2,1,0:T(8,128)(2,1)} copy(bf16[4,45,288]{2,0,1:T(4,128)(2,1)} %param.19) | data formatting | bytes 207360 | tf_op args[9]
  4.0 2.0 %copy.19.wo_any = bf16[641,288]{1,0:T(8,128)(2,1)} copy(bf16[641,288]{0,1:T(8,128)(2,1)} %param.18) | data formatting | bytes 738432 | tf_op args[8]
  6.0 1.9 %copy.15.latent = bf16[2,4,45,641]{3,2,1,0:T(8,128)(2,1)} copy(bf16[2,4,45,641]{3,1,2,0:T(4,128)(2,1)} %param.10) | data formatting | bytes 923040 | tf_op args[0]
  7.9 0.0 copy-start.2
  7.9 3.8 %copy.18.wr_any = bf16[1282,641]{1,0:T(8,128)(2,1)} copy(bf16[1282,641]{0,1:T(8,128)(2,1)} %param.17) | data formatting | bytes 3287048 | tf_op args[7]
  11.8 0.0 copy-done.2
  11.8 4.1 %copy.17.wd_any = bf16[2564,641]{1,0:T(8,128)(2,1)} copy(bf16[2564,641]{0,1:T(8,128)(2,1)S(1)} %copy-done.2) | data formatting | bytes 6574096 | tf_op args[5]
  15.9 110.0 %step.1 = (bf16[2,4,45,641]{3,2,1,0:T(8,128)(2,1)}, bf16[1920,16,128]{2,1,0:T(8,128)(2,1)}) custom-call(bf16[2,4,45,641]{3,2,1,0:T(8,128)(2,1)} %copy.15.latent, s32[2]{0:T(128)} %seeds.1, bf16[64,641]{1,0:T(8,128)(2,1)} %table.1, s32[4]{0:T(128)} %bands.1, bf16[16,4,7,7]{3,2,1,0:T(8,128)(2,1)} %copy.16.basis, bf16[2564,641]{1,0:T(8,128)(2,1)} %copy.17.wd_any, ...), custom_call_target="tpu_custom_call" | custom-call | tf_op jit(solution)/shard_map/step/pallas_call | solution.py:605
  125.9 2.2 %copy.21 = bf16[2,4,45,641]{3,1,2,0:T(4,128)(2,1)} copy(bf16[2,4,45,641]{3,2,1,0:T(8,128)(2,1)} %get-tuple-element.17) | data formatting | bytes 923040
  128.1 0.0 copy-start
  128.1 3.2 %copy-done = bf16[1920,16,128]{2,1,0:T(8,128)(2,1)S(1)} copy-done((bf16[1920,16,128]{2,1,0:T(8,128)(2,1)S(1)}, bf16[1920,16,128]{2,1,0:T(8,128)(2,1)}, u32[]{:S(2)}) %copy-start) | copy-done | bytes 7864344
  131.3 2.7 %unpack.1 = (bf16[2564,641]{1,0:T(8,128)(2,1)S(1)}, bf16[641,1282]{1,0:T(8,128)(2,1)}, bf16[1282,641]{1,0:T(8,128)(2,1)S(1)}, bf16[641,288]{1,0:T(8,128)(2,1)S(1)}) custom-call(bf16[1920,16,128]{2,1,0:T(8,128)(2,1)S(1)} %copy-done), custom_call_target="tpu_custom_call" | custom-call | tf_op jit(solution)/shard_map/unpack/pallas_call | solution.py:630
  134.0 0.0 copy-start.1
  134.0 1.9 %copy-done.1 = bf16[2564,641]{1,0:T(8,128)(2,1)} copy-done((bf16[2564,641]{1,0:T(8,128)(2,1)}, bf16[2564,641]{1,0:T(8,128)(2,1)S(1)}, u32[]{:S(2)}) %copy-start.1) | copy-done | bytes 3287072
  135.8 6.1 %copy.22 = bf16[2564,641]{0,1:T(8,128)(2,1)} copy(bf16[2564,641]{1,0:T(8,128)(2,1)} %copy-done.1) | data formatting | bytes 6574096
  141.9 1.0 copy.24
  142.9 2.4 %copy.23 = bf16[1282,641]{0,1:T(8,128)(2,1)} copy(bf16[1282,641]{1,0:T(8,128)(2,1)S(1)} %get-tuple-element.20) | data formatting | bytes 3287048
Async XLA Ops:
  7.9 3.8 %copy-start.2 = (bf16[2564,641]{0,1:T(8,128)(2,1)S(1)}, bf16[2564,641]{0,1:T(8,128)(2,1)}, u32[]{:S(2)}) copy-start(bf16[2564,641]{0,1:T(8,128)(2,1)} %param.15) | copy-start | bytes 9861148
  128.1 3.2 %copy-start = (bf16[1920,16,128]{2,1,0:T(8,128)(2,1)S(1)}, bf16[1920,16,128]{2,1,0:T(8,128)(2,1)}, u32[]{:S(2)}) copy-start(bf16[1920,16,128]{2,1,0:T(8,128)(2,1)} %get-tuple-element.12.flat) | copy-start | bytes 23592964
  134.0 1.9 %copy-start.1 = (bf16[2564,641]{1,0:T(8,128)(2,1)}, bf16[2564,641]{1,0:T(8,128)(2,1)S(1)}, u32[]{:S(2)}) copy-start(bf16[2564,641]{1,0:T(8,128)(2,1)S(1)} %get-tuple-element.18) | copy-start | bytes 9861148
where the time goes:
time: 146 us; the launch traced here: 145 us
  Pallas kernels  113 us (77%)
  local copies, waits for them, and re-layouts  32 us (22%)
    pallas_call x1, Pallas kernels, per_device(): pl.pallas_call(step_kernel, out_shape=(jax.ShapeDtypeStruct(latent.shape,...  110 us
    unnamed x16, local copies, waits for them, and re-layouts  32 us

commit v1 on v0

v1 whole, which is shorter than its diff:
```python
import functools
import math

import jax
import jax.numpy as jnp
from jax import lax
from jax.experimental import pallas as pl
from jax.experimental.pallas import tpu as pltpu
from jax.sharding import PartitionSpec as P

MESH = pl.DeviceIdType.MESH
f32 = jnp.float32
bf16 = jnp.bfloat16

CH = 641
HID = 1282
OUTC = 288
WIDE = 2564
ROWS = 384
HALF = 192
POINTS = 180
UNITS = 41
AXES = (("x", "y", "z"), ("y", "z", "x"), ("z", "x", "y"))
OFF_EXPAND, OFF_REDUCE, OFF_DECODE, OFF_DISCO, OFF_TAIL = 0, 410, 820, 960, 1780
U_DECODE = 18
TILES = 1824
WAVES = ((0, 160), (960, 144))


def place():
    member, lon = lax.axis_index("member"), lax.axis_index("lon")
    return {
        "x": (member % 2) * 2 + (lon // 2) % 2,
        "y": lon // 4,
        "z": member // 2,
        "c": lon % 2,
    }


def device(at):
    return (at["z"] * 2 + at["x"] // 2, at["y"] * 4 + (at["x"] % 2) * 2 + at["c"])


def moved(at, axis, step):
    there = dict(at)
    size = 2 if axis == "c" else 4
    there[axis] = lax.rem(at[axis] + step + size, size)
    return there


def iota(shape, dim):
    return lax.broadcasted_iota(jnp.int32, shape, dim)


def dot(a, b):
    return jnp.dot(a, b, preferred_element_type=f32)


def dot_nt(a, b):
    return lax.dot_general(a, b, (((1,), (1,)), ((), ())), preferred_element_type=f32)


def flat_tiles(value):
    return value.astype(bf16).reshape(value.shape[0] // 16, 16, 128)


class Copies:
    def __init__(self, send_sems, recv_sems):
        self.send_sems, self.recv_sems, self.count = send_sems, recv_sems, 0
        self.started = []

    def send(self, src, dst, to):
        copy = pltpu.make_async_remote_copy(
            src_ref=src,
            dst_ref=dst,
            send_sem=self.send_sems.at[self.count],
            recv_sem=self.recv_sems.at[self.count],
            device_id=to,
            device_id_type=MESH,
        )
        self.count += 1
        copy.start()
        self.started.append(copy)
        return copy

    def finish(self):
        for copy in self.started:
            copy.wait_send()


def pair_slopes(fv, og, tgt, me_h, lanes, rows):
    lo, width = lanes
    values = [fv[j, rows, lo : lo + width] for j in range(16)]
    sums = [None] * 16

    def slope(d):
        return d * lax.rsqrt(d * d + 0.25)

    for i in range(16):
        for j in range(i + 1, 16):
            s = slope(values[i] - values[j])
            sums[i] = s if sums[i] is None else sums[i] + s
            sums[j] = -s if sums[j] is None else sums[j] - s
    goal = tgt[:, lo : lo + width]
    keep = me_h
    for i in range(16):
        value = slope(values[i] - goal) - sums[i] * (1.0 / 15.0)
        og[i, rows, lo : lo + width] = jnp.where(keep, value, 0.0)


def step_kernel(
    latent,
    seeds,
    table,
    bands,
    basis,
    wd_any,
    we_any,
    wr_any,
    wo_any,
    target,
    lg,
    flat,
    wd,
    we,
    wr,
    wo,
    tk,
    tt,
    wide,
    hs,
    spread,
    hid,
    hid_t,
    gp,
    act,
    mix,
    halo_s,
    halo_r,
    fs,
    fr,
    fv,
    og,
    gs,
    gr,
    tp,
    fg,
    mg,
    pg,
    hg,
    sgs,
    ob,
    back_r,
    grads,
    r0,
    r1,
    r2,
    r3,
    send_sems,
    recv_sems,
    load_sems,
):
    at = place()
    me = lax.axis_index("member")
    lon = lax.axis_index("lon")
    left = (me, lax.rem(lon + 15, 16))
    right = (me, lax.rem(lon + 1, 16))
    core = at["c"]
    copies = Copies(send_sems, recv_sems)

    loads = []
    for i, (src, dst) in enumerate(((wd_any, wd), (we_any, we), (wr_any, wr), (wo_any, wo))):
        load = pltpu.make_async_copy(src, dst, load_sems.at[i])
        load.start()
        loads.append(load)

    sibling = device(moved(at, "c", 1))
    barrier = pltpu.get_barrier_semaphore()
    greet = [sibling, left, right]
    greet += [device(moved(at, axis, d)) for axis in "xyz" for d in (1, 2, 3)]
    greet += [(lax.rem(me + d, 8), lon) for d in range(1, 8)]
    for peer in greet:
        pl.semaphore_signal(barrier, inc=1, device_id=peer, device_id_type=MESH)

    for ref in (hid, mix, mg, hg):
        ref[:, 640:768] = jnp.zeros((ROWS, 128), bf16)
    for ref in (act, pg):
        ref[:, 1280:1408] = jnp.zeros((ROWS, 128), bf16)
    fg[:, 256:384] = jnp.zeros((ROWS, 128), bf16)
    low4 = iota((16, 768), 0) < 4
    for m in range(2):
        pick = jnp.where(iota((8, 64), 1) == seeds[m], 1.0, 0.0).astype(bf16)
        offset = dot(pick, table[...])[0:1]
        value = latent[m].astype(f32).reshape(POINTS, CH) + offset
        value = jnp.concatenate([value, jnp.zeros((POINTS, 127), f32)], axis=1)
        value = jnp.concatenate([value, jnp.zeros((76, 768), f32)], axis=0)
        seeded = value.astype(bf16)
        wide[m] = seeded
        hs[m * HALF : m * HALF + HALF] = seeded[0:HALF]
        first = pltpu.roll(value[0:16], 4, 0)
        final = pltpu.roll(value[160:192], 28, 0)[0:16]
        halo_s[0, m] = jnp.where(low4, 0.0, first).astype(bf16)
        halo_s[1, m] = jnp.where(low4, 0.0, final).astype(bf16)

    pl.semaphore_wait(barrier, len(greet))
    from_right = copies.send(halo_s.at[0], halo_r.at[0], left)
    from_left = copies.send(halo_s.at[1], halo_r.at[1], right)

    line = iota((8, 16), 0) & 3
    chosen = jnp.where(line == 0, bands[0], jnp.where(line == 1, bands[1], bands[2]))
    chosen = jnp.where(line == 3, bands[3], chosen)
    picks = jnp.where(iota((8, 16), 1) == chosen, 1.0, 0.0).astype(bf16)
    taps = dot_nt(picks, basis[...].astype(f32).reshape(196, 16).astype(bf16))
    line = iota((8, 196), 0) & 3
    index = iota((8, 196), 1)
    taps = jnp.where((index >= 28 * (3 - line)) & (index < 28 * (7 - line)), taps, 0.0)
    taps = taps.astype(bf16)
    index = iota((196, 256), 0)
    pair = lax.shift_right_logical(index, 2)
    a = lax.shift_right_logical(pair * 37, 8)
    spot = (4 * (pair - 7 * a) + a + (256 - 15)) & 255
    hit = iota((196, 256), 1) == spot
    sub = iota((8, 256), 0)
    for k in range(4):
        place_k = jnp.where(hit & ((index & 3) == k), 1.0, 0.0).astype(bf16)
        first = pltpu.roll(dot(taps, place_k), 0, 1, stride=1, stride_axis=0)
        lines = [first if i == 0 else pltpu.roll(first, 8 * i, 1) for i in range(23)]
        lines[22] = jnp.where(sub < 4, lines[22], 0.0)
        lines.append(jnp.zeros((8, 256), f32))
        band = jnp.concatenate(lines, axis=0).astype(bf16)
        tk[k] = band
        tt[:, k * HALF : k * HALF + HALF] = band.T
    tp[0:176] = target[0:44].astype(f32).reshape(176, OUTC)
    tp[176:184] = jnp.concatenate(
        [target[44].astype(f32), jnp.zeros((4, OUTC), f32)], axis=0
    )
    tp[184:192] = jnp.zeros((8, OUTC), f32)

    from_right.wait_recv()
    from_left.wait_recv()
    for m in range(2):
        wide[m, 176:192] = wide[m, 176:192] + halo_r[0, m]
        wide[m, 240:256] = halo_r[1, m]

    for m in range(2):
        carry = None
        rows = slice(m * HALF, m * HALF + HALF)
        for k in range(4):
            value = dot(tk[k], wide[m])
            if k:
                value = pltpu.roll(value, k, 1)
            head = value[:, 0:128] if carry is None else value[:, 0:128] + carry
            spread[rows, 640 * k : 640 * k + 128] = head.astype(bf16)
            spread[rows, 640 * k + 128 : 640 * k + 640] = value[:, 128:640].astype(bf16)
            carry = value[:, 640:768]
        spread[rows, 2560:2688] = carry.astype(bf16)

    for load in loads:
        load.wait()
    conv = dot_nt(spread[:, 0:WIDE], wd[...])
    hid[:, 0:CH] = (hs[:, 0:CH].astype(f32) + conv).astype(bf16)
    pre = dot(hid[:, 0:CH], we[...])
    inner = math.sqrt(2.0 / math.pi)
    square = pre * pre
    t = jnp.tanh(inner * (pre + 0.044715 * (square * pre)))
    act[:, 0:HID] = (0.5 * pre * (1.0 + t)).astype(bf16)
    gp[...] = 0.5 * (1.0 + t) + (0.5 * inner) * pre * (1.0 - t * t) * (
        1.0 + (3.0 * 0.044715) * square
    )
    mix[:, 0:CH] = (hid[:, 0:CH].astype(f32) + dot_nt(act[:, 0:HID], wr[...])).astype(bf16)
    fields = dot_nt(mix[:, 0:CH], wo[...])
    for p in range(8):
        block = jnp.concatenate(
            [fields[24 * p : 24 * p + 24], fields[HALF + 24 * p : HALF + 24 * p + 24]], axis=0
        )
        fs[p] = block.astype(bf16)
    there = []
    for d in range(1, 8):
        peer = lax.rem(me + d, 8)
        there.append(copies.send(fs.at[peer], fr.at[me], (peer, lon)))
    fr[me] = fs[me]
    hid_t[...] = hid[...].T

    for copy in there:
        copy.wait_recv()
    for p in range(8):
        block = fr[p].astype(f32)
        fv[2 * p] = block[0:24]
        fv[2 * p + 1] = block[24:48]

    def slopes(i, carry):
        start = pl.multiple_of(i * 8, 8)
        rows = pl.ds(start, 8)
        goal = tp[pl.ds(pl.multiple_of(me * 24 + start, 8), 8), :]
        for lanes in ((0, 128), (128, 128), (256, 32)):
            keep = iota((8, lanes[1]), 0) + (me * 24 + start) < POINTS
            pair_slopes(fv, og, goal, keep, lanes, rows)
        return carry

    lax.fori_loop(0, 3, slopes, 0)
    for p in range(8):
        gs[p] = jnp.concatenate([og[2 * p], og[2 * p + 1]], axis=0).astype(bf16)
    back = []
    for d in range(1, 8):
        peer = lax.rem(me + d, 8)
        back.append(copies.send(gs.at[peer], gr.at[me], (peer, lon)))
    gr[me] = gs[me]
    for copy in back:
        copy.wait_recv()
    blocks = [gr[p].astype(f32) for p in range(8)]
    fg[:, 0:OUTC] = jnp.concatenate(
        [b[0:24] for b in blocks] + [b[24:48] for b in blocks], axis=0
    ).astype(bf16)

    factor = 1.0 / math.sqrt(46080.0)

    def add_tiles(dst, dst_at, parts, count, step, scale=None):
        def body(i, carry):
            total = None
            for ref, start in parts:
                piece = ref[pl.ds(start + i * step, step)].astype(f32)
                total = piece if total is None else total + piece
            if scale is not None:
                total = total * scale
            dst[pl.ds(dst_at + i * step, step)] = total.astype(bf16)
            return carry

        lax.fori_loop(0, count // step, body, 0)

    def reduced(wave, p):
        base, size = WAVES[wave]
        sa, sb = size // 4, size // 16
        start = base + 2 * p * size
        mine = start + core * size
        first, second, third = AXES[p]
        mine_a = mine + at[first] * sa
        mine_b = mine_a + at[second] * sb
        lane = (0 if wave == 0 else 480) + p * size
        r0_at = lane
        lane_a = (0 if wave == 0 else 360) + p * 3 * sa
        lane_b = (0 if wave == 0 else 90) + p * 3 * sb
        lane_c = (0 if wave == 0 else 120) + p * 4 * sb

        def to_peers(axis, src, dst):
            return [
                copies.send(src(d, moved(at, axis, d)), dst(d), device(moved(at, axis, d)))
                for d in (1, 3, 2)
            ]

        across = copies.send(
            grads.at[pl.ds(start + (1 - core) * size, size)],
            r0.at[pl.ds(r0_at, size)],
            sibling,
        )
        yield
        across.wait_recv()
        add_tiles(grads, mine, [(grads, mine), (r0, r0_at)], size, 16)
        sent = to_peers(
            first,
            lambda d, to: grads.at[pl.ds(mine + to[first] * sa, sa)],
            lambda d: r1.at[pl.ds(lane_a + (d - 1) * sa, sa)],
        )
        yield
        for copy in sent:
            copy.wait_recv()
        add_tiles(
            grads, mine_a, [(grads, mine_a)] + [(r1, lane_a + d * sa) for d in range(3)], sa, sb
        )
        sent = to_peers(
            second,
            lambda d, to: grads.at[pl.ds(mine_a + to[second] * sb, sb)],
            lambda d: r2.at[pl.ds(lane_b + (d - 1) * sb, sb)],
        )
        yield
        for copy in sent:
            copy.wait_recv()
        add_tiles(
            grads, mine_b, [(grads, mine_b)] + [(r2, lane_b + d * sb) for d in range(3)], sb, sb
        )
        own = pl.ds(lane_c + at[third] * sb, sb)
        sent = to_peers(
            third, lambda d, to: grads.at[pl.ds(mine_b, sb)], lambda d: r3.at[own]
        )
        r3[own] = grads[pl.ds(mine_b, sb)]
        yield
        for copy in sent:
            copy.wait_recv()
        add_tiles(flat, mine_b, [(r3, lane_c + q * sb) for q in range(4)], sb, sb, factor)
        region_b = flat.at[pl.ds(mine_b, sb)]
        sent = to_peers(second, lambda d, to: region_b, lambda d: region_b)
        yield
        for copy in sent:
            copy.wait_recv()
        region_a = flat.at[pl.ds(mine_a, sa)]
        sent = to_peers(first, lambda d, to: region_a, lambda d: region_a)
        last = [copies.send(region_a, region_a, sibling)]
        yield
        for d, copy in zip((1, 3, 2), sent):
            copy.wait_recv()
            came = lax.rem(at[first] + 4 - d, 4)
            region = flat.at[pl.ds(mine + came * sa, sa)]
            last.append(copies.send(region, region, sibling))
        yield
        for copy in last:
            copy.wait_recv()
        yield

    one = [reduced(0, p) for p in range(3)]
    two = [reduced(1, p) for p in range(3)]

    def advance(wave):
        for part in wave:
            next(part)

    def put_columns(value, off, units, count):
        for j in range(count):
            grads[pl.ds(off + j * units, units)] = flat_tiles(
                value[0 : units * 16, 128 * j : 128 * j + 128]
            )

    mixed_grad = dot(fg[:, 0:OUTC], wo[...])
    mg[:, 0:CH] = mixed_grad.astype(bf16)
    pg[:, 0:HID] = (dot(mg[:, 0:CH], wr[...]) * gp[...]).astype(bf16)

    value = dot(hid_t[0:656], pg[...])
    put_columns(value, OFF_EXPAND, UNITS, 10)
    tail = pltpu.roll(value[:, 1280:1408], 4, 1)
    value = dot(mg[...].T[0:656], act[...])
    put_columns(value, OFF_REDUCE, UNITS, 10)
    tail = tail + pltpu.roll(value[:, 1280:1408], 6, 1)
    value = dot(fg[...].T[0:OUTC], mix[...])
    put_columns(value, OFF_DECODE, U_DECODE, 5)
    last_lane = jnp.concatenate([value[:, 640:768], jnp.zeros((656 - OUTC, 128), f32)], axis=0)
    tail = tail + pltpu.roll(last_lane, 8, 1)
    advance(one)

    hidden_grad = mg[:, 0:CH].astype(f32) + dot_nt(pg[:, 0:HID], we[...])
    hg[:, 0:CH] = hidden_grad.astype(bf16)
    hg_t = hg[...].T[0:656]
    for c in range(5):
        value = dot(hg_t, spread[:, 512 * c : 512 * c + 512])
        put_columns(value, OFF_DISCO + 4 * c * UNITS, UNITS, 4)
        if c == 1:
            advance(one)
    tail = tail + dot(hg_t, spread[:, 2560:2688])
    put_columns(tail, OFF_TAIL, UNITS, 1)
    advance(two)

    for m in range(2):
        rows = slice(m * HALF, m * HALF + HALF)
        value = dot(hg[rows, 0:CH], wd[...]).astype(bf16).astype(f32)
        value = jnp.concatenate([value, jnp.zeros((HALF, 124), f32)], axis=1)
        for k in range(4):
            piece = value[:, 640 * k : 640 * k + 768]
            if k:
                piece = pltpu.roll(piece, 768 - k, 1)
            sgs[k * HALF : k * HALF + HALF, :] = piece[:, 0:CH].astype(bf16)
        if m == 0:
            advance(two)
        out = dot(tt[...], sgs[...])
        ob[0, m] = out[240:256]
        ob[1, m] = out[176:192]
        gp[rows, 0:CH] = hg[rows, 0:CH].astype(f32) + out[0:HALF]
    to_left = copies.send(ob.at[0], back_r.at[0], left)
    to_right = copies.send(ob.at[1], back_r.at[1], right)
    advance(one)
    advance(one)
    to_left.wait_recv()
    to_right.wait_recv()
    low = iota((16, CH), 0)
    for m in range(2):
        base = m * HALF
        after = pltpu.roll(back_r[1, m], 12, 0)
        gp[base : base + 16, 0:CH] = gp[base : base + 16, 0:CH] + jnp.where(low < 12, after, 0.0)
        before = jnp.where(low >= 4, back_r[0, m], 0.0)
        before = jnp.concatenate([before, jnp.zeros((16, CH), f32)], axis=0)
        before = pltpu.roll(before, 4, 0)
        spot = slice(base + 160, base + 192)
        gp[spot, 0:CH] = gp[spot, 0:CH] + before
        total = gp[base : base + HALF, 0:CH]
        lg[m] = total[0:POINTS].reshape(45, 4, CH).astype(bf16)
    advance(two)
    advance(one)
    advance(two)
    advance(one)
    advance(two)
    advance(one)
    advance(two)
    advance(two)
    advance(one)
    advance(two)
    copies.finish()


def unpack_kernel(flat, disco, expand, reduce, decode):
    def column(start, units):
        return flat[start : start + units].reshape(units * 16, 128)

    tail = column(OFF_TAIL, UNITS)
    wide_tail = tail.astype(f32)
    for j in range(20):
        disco[:, 128 * j : 128 * j + 128] = column(OFF_DISCO + j * UNITS, UNITS)[0:CH]
    disco[:, 2560:WIDE] = tail[0:CH, 0:4]
    for j in range(10):
        expand[:, 128 * j : 128 * j + 128] = column(OFF_EXPAND + j * UNITS, UNITS)[0:CH]
        reduce[:, 128 * j : 128 * j + 128] = column(OFF_REDUCE + j * UNITS, UNITS)[0:CH]
    expand[:, 1280:HID] = pltpu.roll(wide_tail, 124, 1)[0:CH, 0:2].astype(bf16)
    reduce[:, 1280:HID] = pltpu.roll(wide_tail, 122, 1)[0:CH, 0:2].astype(bf16)
    for j in range(5):
        decode[:, 128 * j : 128 * j + 128] = column(OFF_DECODE + j * U_DECODE, U_DECODE)
    decode[:, 640:CH] = pltpu.roll(wide_tail, 120, 1)[0:OUTC, 0:1].astype(bf16)


def per_device(
    latent,
    member_seeds,
    member_table,
    row_bands,
    disco_basis,
    w_disco,
    w_expand,
    w_reduce,
    w_decode,
    target,
):
    vm = pl.BlockSpec(memory_space=pltpu.VMEM)
    sm = pl.BlockSpec(memory_space=pltpu.SMEM)
    anywhere = pl.BlockSpec(memory_space=pl.ANY)
    V = pltpu.VMEM
    copies = 150
    scratch = [
        V((CH, WIDE), bf16),
        V((CH, HID), bf16),
        V((CH, HID), bf16),
        V((OUTC, CH), bf16),
        V((4, HALF, 256), bf16),
        V((256, 768), bf16),
        V((2, 256, 768), bf16),
        V((ROWS, 768), bf16),
        V((ROWS, 2688), bf16),
        V((ROWS, 768), bf16),
        V((768, ROWS), bf16),
        V((ROWS, HID), f32),
        V((ROWS, 1408), bf16),
        V((ROWS, 768), bf16),
        V((2, 2, 16, 768), bf16),
        V((2, 2, 16, 768), bf16),
        V((8, 48, OUTC), bf16),
        V((8, 48, OUTC), bf16),
        V((16, 24, OUTC), f32),
        V((16, 24, OUTC), f32),
        V((8, 48, OUTC), bf16),
        V((8, 48, OUTC), bf16),
        V((HALF, OUTC), f32),
        V((ROWS, 384), bf16),
        V((ROWS, 768), bf16),
        V((ROWS, 1408), bf16),
        V((ROWS, 768), bf16),
        V((768, CH), bf16),
        V((2, 2, 16, CH), f32),
        V((2, 2, 16, CH), f32),
        V((TILES, 16, 128), bf16),
        V((912, 16, 128), bf16),
        V((684, 16, 128), bf16),
        V((171, 16, 128), bf16),
        V((228, 16, 128), bf16),
        pltpu.SemaphoreType.DMA((copies,)),
        pltpu.SemaphoreType.DMA((copies,)),
        pltpu.SemaphoreType.DMA((4,)),
    ]
    lg, flat = pl.pallas_call(
        step_kernel,
        out_shape=(
            jax.ShapeDtypeStruct((2, 45, 4, CH), bf16),
            jax.ShapeDtypeStruct((TILES, 16, 128), bf16),
        ),
        in_specs=[vm, sm, vm, sm, vm, anywhere, anywhere, anywhere, anywhere, vm],
        out_specs=(vm, vm),
        scratch_shapes=scratch,
        compiler_params=pltpu.CompilerParams(
            collective_id=0, has_side_effects=True, vmem_limit_bytes=54_000_000
        ),
        name="step",
    )(
        latent.transpose(0, 2, 1, 3),
        member_seeds,
        member_table,
        row_bands,
        disco_basis.transpose(2, 3, 1, 0),
        w_disco.T,
        w_expand,
        w_reduce.T,
        w_decode.T,
        target.transpose(1, 0, 2),
    )
    disco, expand, reduce, decode = pl.pallas_call(
        unpack_kernel,
        out_shape=(
            jax.ShapeDtypeStruct((CH, WIDE), bf16),
            jax.ShapeDtypeStruct((CH, HID), bf16),
            jax.ShapeDtypeStruct((CH, HID), bf16),
            jax.ShapeDtypeStruct((OUTC, CH), bf16),
        ),
        in_specs=[vm],
        out_specs=(vm, vm, vm, vm),
        compiler_params=pltpu.CompilerParams(vmem_limit_bytes=30_000_000),
        name="unpack",
    )(flat)
    return (lg.transpose(0, 2, 1, 3), disco.T, expand, reduce.T, decode.T)


def solution(mesh):
    placed = (
        P("member", None, "lon", None),
        P("member"),
        P(),
        P(),
        P(),
        P(),
        P(),
        P(),
        P(),
        P(None, "lon", None),
    )
    return jax.shard_map(
        per_device,
        mesh=mesh,
        in_specs=placed,
        out_specs=(P("member", None, "lon", None), P(), P(), P(), P()),
        check_vma=False,
    )
```

time: 146 us -> 107 us (0.73)
  local copies, waits for them, and re-layouts: 32 us -> 9.88 us
  Pallas kernels: 113 us -> 96.6 us
    unnamed x16 -> x17, local copies, waits for them, and re-layouts: 32 us -> 9.88 us
    pallas_call x2, Pallas kernels: 113 us -> 96.6 us  [the longest x1 93.1 us: per_device(): pl.pallas_call(step_kernel, out_shape=(jax.ShapeDtypeStruct((2, 45, 4, CH...]
where the time goes in v1:
time: 107 us
  Pallas kernels  96.6 us (90%)
  local copies, waits for them, and re-layouts  9.88 us (9%)
    pallas_call x1, Pallas kernels, per_device(): pl.pallas_call(step_kernel, out_shape=(jax.ShapeDtypeStruct((2, 45, 4, CH...  93.1 us
    unnamed x17, local copies, waits for them, and re-layouts  9.88 us
    pallas_call x1, Pallas kernels, per_device(): pl.pallas_call(unpack_kernel, out_shape=(jax.ShapeDtypeStruct((CH, WIDE),...  3.48 us

profile of v1, /device:TPU:1, one launch (start us, length us, event | category | flops | bytes accessed | tf_op | source)
XLA Modules:
  0.0 107.1 jit_solution(16472115268619940472)
XLA Ops:
  0.6 0.0 copy-start.1
  0.6 1.0 copy-done.1
  1.7 0.0 copy-start.2
  1.7 1.0 copy-done.2
  2.7 0.0 copy-start.3
  2.7 0.9 copy-done.3
  3.6 0.0 copy-start.4
  3.6 0.9 copy-done.4
  4.5 0.0 copy-start.5
  4.5 0.8 copy-done.5
  5.3 0.0 copy-start.6
  5.3 0.7 copy-done.6
  6.0 0.0 copy-start.7
  6.0 0.7 copy-done.7
  6.6 93.1 %step.1 = (bf16[2,45,4,641]{3,2,1,0:T(4,128)(2,1)S(1)}, bf16[1824,16,128]{2,1,0:T(8,128)(2,1)}) custom-call(bf16[2,45,4,641]{3,2,1,0:T(4,128)(2,1)S(1)} %bitcast.11, s32[2]{0:T(128)S(1)} %copy-done.6, bf16[64,641]{1,0:T(8,128)(2,1)S(1)} %copy-done.4, s32[4]{0:T(128)S(1)} %copy-done.7, bf16[7,7,4,16]{3,2,1,0:T(4,128)(2,1)S(1)} %bitcast.14, ...), custom_call_target="tpu_custom_call" | custom-call | tf_op jit(solution)/shard_map/step/pallas_call | solution.py:571
  99.7 0.0 copy-start
  99.7 3.1 %copy-done = bf16[1824,16,128]{2,1,0:T(8,128)(2,1)S(1)} copy-done((bf16[1824,16,128]{2,1,0:T(8,128)(2,1)S(1)}, bf16[1824,16,128]{2,1,0:T(8,128)(2,1)}, u32[]{:S(2)}) %copy-start) | copy-done | bytes 7471128
  102.8 3.5 %unpack.1 = (bf16[641,2564]{1,0:T(8,128)(2,1)}, bf16[641,1282]{1,0:T(8,128)(2,1)}, bf16[641,1282]{1,0:T(8,128)(2,1)}, bf16[288,641]{1,0:T(8,128)(2,1)}) custom-call(bf16[1824,16,128]{2,1,0:T(8,128)(2,1)S(1)} %copy-done), custom_call_target="tpu_custom_call" | custom-call | tf_op jit(solution)/shard_map/unpack/pallas_call | solution.py:596
  106.3 0.8 copy.16
Async XLA Ops:
  0.6 1.1 copy-start.1
  1.7 1.0 copy-start.2
  2.7 0.9 copy-start.3
  3.6 0.9 copy-start.4
  4.5 0.8 copy-start.5
  5.3 0.7 copy-start.6
  6.0 0.7 copy-start.7
  99.7 3.1 %copy-start = (bf16[1824,16,128]{2,1,0:T(8,128)(2,1)S(1)}, bf16[1824,16,128]{2,1,0:T(8,128)(2,1)}, u32[]{:S(2)}) copy-start(bf16[1824,16,128]{2,1,0:T(8,128)(2,1)} %get-tuple-element.12.flat) | copy-start | bytes 22413316

commit v2 on v1

--- a/solution.py
+++ b/solution.py
@@ -109,18 +109,25 @@
 
 
 def step_kernel(
+    latent_any,
+    seeds_any,
+    table_any,
+    bands_any,
+    basis_any,
+    wd_any,
+    we_any,
+    wr_any,
+    wo_any,
+    target_any,
+    lg,
+    flat_any,
+    flat,
     latent,
     seeds,
     table,
     bands,
     basis,
-    wd_any,
-    we_any,
-    wr_any,
-    wo_any,
     target,
-    lg,
-    flat,
     wd,
     we,
     wr,
@@ -159,6 +166,7 @@
     send_sems,
     recv_sems,
     load_sems,
+    store_sems,
 ):
     at = place()
     me = lax.axis_index("member")
@@ -168,6 +176,20 @@
     core = at["c"]
     copies = Copies(send_sems, recv_sems)
 
+    early = []
+    for i, (src, dst) in enumerate(
+        (
+            (latent_any, latent),
+            (seeds_any, seeds),
+            (table_any, table),
+            (bands_any, bands),
+            (basis_any, basis),
+            (target_any, target),
+        )
+    ):
+        load = pltpu.make_async_copy(src, dst, load_sems.at[4 + i])
+        load.start()
+        early.append(load)
     loads = []
     for i, (src, dst) in enumerate(((wd_any, wd), (we_any, we), (wr_any, wr), (wo_any, wo))):
         load = pltpu.make_async_copy(src, dst, load_sems.at[i])
@@ -188,6 +210,8 @@
         ref[:, 1280:1408] = jnp.zeros((ROWS, 128), bf16)
     fg[:, 256:384] = jnp.zeros((ROWS, 128), bf16)
     low4 = iota((16, 768), 0) < 4
+    for load in early:
+        load.wait()
     for m in range(2):
         pick = jnp.where(iota((8, 64), 1) == seeds[m], 1.0, 0.0).astype(bf16)
         offset = dot(pick, table[...])[0:1]
@@ -313,6 +337,13 @@
     ).astype(bf16)
 
     factor = 1.0 / math.sqrt(46080.0)
+    stores = []
+
+    def store(start, count):
+        spot = pl.ds(start, count)
+        copy = pltpu.make_async_copy(flat.at[spot], flat_any.at[spot], store_sems.at[len(stores)])
+        copy.start()
+        stores.append(copy)
 
     def add_tiles(dst, dst_at, parts, count, step, scale=None):
         def body(i, carry):
@@ -347,6 +378,15 @@
                 for d in (1, 3, 2)
             ]
 
+        half = sa // 2
+        onward, backward = device(moved(at, first, 1)), device(moved(at, first, 3))
+
+        def block(step, side):
+            return mine + lax.rem(at[first] + step, 4) * sa + side * half
+
+        def landing(step):
+            return lane_a + step * half
+
         across = copies.send(
             grads.at[pl.ds(start + (1 - core) * size, size)],
             r0.at[pl.ds(r0_at, size)],
@@ -355,16 +395,25 @@
         yield
         across.wait_recv()
         add_tiles(grads, mine, [(grads, mine), (r0, r0_at)], size, 16)
-        sent = to_peers(
-            first,
-            lambda d, to: grads.at[pl.ds(mine + to[first] * sa, sa)],
-            lambda d: r1.at[pl.ds(lane_a + (d - 1) * sa, sa)],
-        )
+
+        def give(at_tile, step, to):
+            return copies.send(grads.at[pl.ds(at_tile, half)], r1.at[pl.ds(landing(step), half)], to)
+
+        relay_on = give(block(2, 0), 4, onward)
+        relay_back = give(block(2, 1), 5, backward)
+        sent = [give(block(1, 1), 1, onward), give(block(3, 0), 2, backward)]
+        yield
+        relay_on.wait_recv()
+        add_tiles(grads, block(1, 0), [(grads, block(1, 0)), (r1, landing(4))], half, half)
+        sent.append(give(block(1, 0), 0, onward))
+        relay_back.wait_recv()
+        add_tiles(grads, block(3, 1), [(grads, block(3, 1)), (r1, landing(5))], half, half)
+        sent.append(give(block(3, 1), 3, backward))
         yield
         for copy in sent:
             copy.wait_recv()
         add_tiles(
-            grads, mine_a, [(grads, mine_a)] + [(r1, lane_a + d * sa) for d in range(3)], sa, sb
+            grads, mine_a, [(grads, mine_a)] + [(r1, lane_a + d * sa) for d in range(2)], sa, sb
         )
         sent = to_peers(
             second,
@@ -391,18 +440,40 @@
         yield
         for copy in sent:
             copy.wait_recv()
-        region_a = flat.at[pl.ds(mine_a, sa)]
-        sent = to_peers(first, lambda d, to: region_a, lambda d: region_a)
-        last = [copies.send(region_a, region_a, sibling)]
-        yield
-        for d, copy in zip((1, 3, 2), sent):
+
+        def pass_on(step, side, to):
+            region = flat.at[pl.ds(block(step, side), half)]
+            return copies.send(region, region, to)
+
+        def share(step):
+            region = flat.at[pl.ds(block(step, 0), sa)]
+            copy = copies.send(region, region, sibling)
+            store(block(step, 0), sa)
+            return copy
+
+        from_before = pass_on(0, 0, onward)
+        from_after = pass_on(0, 1, backward)
+        rest_before = pass_on(0, 1, onward)
+        rest_after = pass_on(0, 0, backward)
+        last = [share(0)]
+        yield
+        from_before.wait_recv()
+        far_before = pass_on(3, 0, onward)
+        from_after.wait_recv()
+        far_after = pass_on(1, 1, backward)
+        yield
+        rest_before.wait_recv()
+        last.append(share(3))
+        rest_after.wait_recv()
+        last.append(share(1))
+        yield
+        far_before.wait_recv()
+        far_after.wait_recv()
+        last.append(share(2))
+        yield
+        for step, copy in zip((0, 3, 1, 2), last):
             copy.wait_recv()
-            came = lax.rem(at[first] + 4 - d, 4)
-            region = flat.at[pl.ds(mine + came * sa, sa)]
-            last.append(copies.send(region, region, sibling))
-        yield
-        for copy in last:
-            copy.wait_recv()
+            store(block(step, 0) + (1 - 2 * core) * size, sa)
         yield
 
     one = [reduced(0, p) for p in range(3)]
@@ -457,13 +528,14 @@
             sgs[k * HALF : k * HALF + HALF, :] = piece[:, 0:CH].astype(bf16)
         if m == 0:
             advance(two)
+            advance(one)
         out = dot(tt[...], sgs[...])
         ob[0, m] = out[240:256]
         ob[1, m] = out[176:192]
         gp[rows, 0:CH] = hg[rows, 0:CH].astype(f32) + out[0:HALF]
     to_left = copies.send(ob.at[0], back_r.at[0], left)
     to_right = copies.send(ob.at[1], back_r.at[1], right)
-    advance(one)
+    advance(two)
     advance(one)
     to_left.wait_recv()
     to_right.wait_recv()
@@ -480,35 +552,78 @@
         total = gp[base : base + HALF, 0:CH]
         lg[m] = total[0:POINTS].reshape(45, 4, CH).astype(bf16)
     advance(two)
-    advance(one)
-    advance(two)
-    advance(one)
-    advance(two)
-    advance(one)
-    advance(two)
-    advance(two)
-    advance(one)
-    advance(two)
+    for _ in range(7):
+        advance(one)
+        advance(two)
+    for copy in stores:
+        copy.wait()
     copies.finish()
 
 
-def unpack_kernel(flat, disco, expand, reduce, decode):
+def unpack_kernel(
+    flat_any,
+    lg_any,
+    disco_any,
+    expand_any,
+    reduce_any,
+    decode_any,
+    lg_out,
+    flat,
+    disco,
+    expand,
+    reduce,
+    decode,
+    lg,
+    in_sems,
+    out_sems,
+):
+    pieces = [(OFF_TAIL, UNITS), (OFF_EXPAND, 410), (OFF_REDUCE, 410), (OFF_DECODE, 90)]
+    pieces += [(OFF_DISCO + 205 * q, 205) for q in range(4)]
+    loads = []
+    for i, (start, count) in enumerate(pieces):
+        spot = pl.ds(start, count)
+        loads.append(pltpu.make_async_copy(flat_any.at[spot], flat.at[spot], in_sems.at[i]))
+        loads[-1].start()
+    loads.append(pltpu.make_async_copy(lg_any, lg, in_sems.at[8]))
+    loads[-1].start()
+    stores = []
+
+    def store(src, dst):
+        stores.append(pltpu.make_async_copy(src, dst, out_sems.at[len(stores)]))
+        stores[-1].start()
+
     def column(start, units):
         return flat[start : start + units].reshape(units * 16, 128)
 
+    loads[0].wait()
     tail = column(OFF_TAIL, UNITS)
     wide_tail = tail.astype(f32)
-    for j in range(20):
-        disco[:, 128 * j : 128 * j + 128] = column(OFF_DISCO + j * UNITS, UNITS)[0:CH]
-    disco[:, 2560:WIDE] = tail[0:CH, 0:4]
+    loads[1].wait()
     for j in range(10):
         expand[:, 128 * j : 128 * j + 128] = column(OFF_EXPAND + j * UNITS, UNITS)[0:CH]
+    expand[:, 1280:HID] = pltpu.roll(wide_tail, 124, 1)[0:CH, 0:2].astype(bf16)
+    store(expand, expand_any)
+    loads[2].wait()
+    for j in range(10):
         reduce[:, 128 * j : 128 * j + 128] = column(OFF_REDUCE + j * UNITS, UNITS)[0:CH]
-    expand[:, 1280:HID] = pltpu.roll(wide_tail, 124, 1)[0:CH, 0:2].astype(bf16)
     reduce[:, 1280:HID] = pltpu.roll(wide_tail, 122, 1)[0:CH, 0:2].astype(bf16)
+    store(reduce, reduce_any)
+    loads[3].wait()
     for j in range(5):
         decode[:, 128 * j : 128 * j + 128] = column(OFF_DECODE + j * U_DECODE, U_DECODE)
     decode[:, 640:CH] = pltpu.roll(wide_tail, 120, 1)[0:OUTC, 0:1].astype(bf16)
+    store(decode, decode_any)
+    disco[:, 2560:WIDE] = tail[0:CH, 0:4]
+    for q in range(4):
+        loads[4 + q].wait()
+        for j in range(5 * q, 5 * q + 5):
+            disco[:, 128 * j : 128 * j + 128] = column(OFF_DISCO + j * UNITS, UNITS)[0:CH]
+        spot = slice(640 * q, WIDE if q == 3 else 640 * q + 640)
+        store(disco.at[:, spot], disco_any.at[:, spot])
+    loads[8].wait()
+    store(lg, lg_out)
+    for copy in stores:
+        copy.wait()
 
 
 def per_device(
@@ -524,11 +639,17 @@
     target,
 ):
     vm = pl.BlockSpec(memory_space=pltpu.VMEM)
-    sm = pl.BlockSpec(memory_space=pltpu.SMEM)
-    anywhere = pl.BlockSpec(memory_space=pl.ANY)
+    hbm = pl.BlockSpec(memory_space=pltpu.HBM)
     V = pltpu.VMEM
-    copies = 150
+    copies = 180
     scratch = [
+        V((TILES, 16, 128), bf16),
+        V((2, 45, 4, CH), bf16),
+        pltpu.SMEM((2,), jnp.int32),
+        V((64, CH), bf16),
+        pltpu.SMEM((4,), jnp.int32),
+        V((7, 7, 4, 16), bf16),
+        V((45, 4, OUTC), bf16),
         V((CH, WIDE), bf16),
         V((CH, HID), bf16),
         V((CH, HID), bf16),
@@ -566,7 +687,8 @@
         V((228, 16, 128), bf16),
         pltpu.SemaphoreType.DMA((copies,)),
         pltpu.SemaphoreType.DMA((copies,)),
-        pltpu.SemaphoreType.DMA((4,)),
+        pltpu.SemaphoreType.DMA((10,)),
+        pltpu.SemaphoreType.DMA((48,)),
     ]
     lg, flat = pl.pallas_call(
         step_kernel,
@@ -574,11 +696,11 @@
             jax.ShapeDtypeStruct((2, 45, 4, CH), bf16),
             jax.ShapeDtypeStruct((TILES, 16, 128), bf16),
         ),
-        in_specs=[vm, sm, vm, sm, vm, anywhere, anywhere, anywhere, anywhere, vm],
-        out_specs=(vm, vm),
+        in_specs=[hbm] * 10,
+        out_specs=(vm, hbm),
         scratch_shapes=scratch,
         compiler_params=pltpu.CompilerParams(
-            collective_id=0, has_side_effects=True, vmem_limit_bytes=54_000_000
+            collective_id=0, has_side_effects=True, vmem_limit_bytes=67_000_000
         ),
         name="step",
     )(
@@ -593,19 +715,18 @@
         w_decode.T,
         target.transpose(1, 0, 2),
     )
-    disco, expand, reduce, decode = pl.pallas_call(
+    shapes = ((CH, WIDE), (CH, HID), (CH, HID), (OUTC, CH), (2, 45, 4, CH))
+    disco, expand, reduce, decode, lg = pl.pallas_call(
         unpack_kernel,
-        out_shape=(
-            jax.ShapeDtypeStruct((CH, WIDE), bf16),
-            jax.ShapeDtypeStruct((CH, HID), bf16),
-            jax.ShapeDtypeStruct((CH, HID), bf16),
-            jax.ShapeDtypeStruct((OUTC, CH), bf16),
-        ),
-        in_specs=[vm],
-        out_specs=(vm, vm, vm, vm),
-        compiler_params=pltpu.CompilerParams(vmem_limit_bytes=30_000_000),
+        out_shape=tuple(jax.ShapeDtypeStruct(shape, bf16) for shape in shapes),
+        in_specs=[hbm, hbm],
+        out_specs=(hbm,) * 5,
+        scratch_shapes=[V((TILES, 16, 128), bf16)]
+        + [V(shape, bf16) for shape in shapes]
+        + [pltpu.SemaphoreType.DMA((9,)), pltpu.SemaphoreType.DMA((8,))],
+        compiler_params=pltpu.CompilerParams(vmem_limit_bytes=67_000_000),
         name="unpack",
-    )(flat)
+    )(flat, lg)
     return (lg.transpose(0, 2, 1, 3), disco.T, expand, reduce.T, decode.T)
 
 

time: 107 us -> 91.8 us (0.86)
  local copies, waits for them, and re-layouts: 9.88 us -> 0 us
  Pallas kernels: 96.6 us -> 90.9 us
    unnamed x17 -> x0, local copies, waits for them, and re-layouts: 9.88 us -> none
    pallas_call x1, Pallas kernels: 93.1 us -> 85.5 us  [per_device(): pl.pallas_call(step_kernel, out_shape=(jax.ShapeDtypeStruct((2, 45, 4, CH...]
    pallas_call x1, Pallas kernels: 3.48 us -> 5.39 us  [per_device(): pl.pallas_call(unpack_kernel, out_shape=tuple((jax.ShapeDtypeStruct(shape...]
where the time goes in v2:
time: 91.8 us; the launch traced here: 91.7 us
  Pallas kernels  90.9 us (99%)
    pallas_call x1, Pallas kernels, per_device(): pl.pallas_call(step_kernel, out_shape=(jax.ShapeDtypeStruct((2, 45, 4, CH...  85.5 us
    pallas_call x1, Pallas kernels, per_device(): pl.pallas_call(unpack_kernel, out_shape=tuple((jax.ShapeDtypeStruct(shape...  5.39 us

profile of v2, /device:TPU:1, one launch (start us, length us, event | category | flops | bytes accessed | tf_op | source)
XLA Modules:
  0.0 91.7 jit_solution(14784470100573897728)
XLA Ops:
  0.6 85.5 %step.1 = (bf16[2,45,4,641]{3,2,1,0:T(4,128)(2,1)}, bf16[1824,16,128]{2,1,0:T(8,128)(2,1)}) custom-call(bf16[2,45,4,641]{3,2,1,0:T(4,128)(2,1)} %bitcast.12, s32[2]{0:T(128)} %seeds_any.1, bf16[64,641]{1,0:T(8,128)(2,1)} %table_any.1, s32[4]{0:T(128)} %bands_any.1, bf16[7,7,4,16]{3,2,1,0:T(4,128)(2,1)} %bitcast.15, bf16[641,2564]{1,0:T(8,128)(2,1)} %bitcast.10, ...), custom_call_target="tpu_custom_call" | custom-call | tf_op jit(solution)/shard_map/step/pallas_call | solution.py:693
  86.1 5.4 %unpack.1 = (bf16[641,2564]{1,0:T(8,128)(2,1)}, bf16[641,1282]{1,0:T(8,128)(2,1)}, bf16[641,1282]{1,0:T(8,128)(2,1)}, bf16[288,641]{1,0:T(8,128)(2,1)}, bf16[2,45,4,641]{3,2,1,0:T(4,128)(2,1)}) custom-call(bf16[1824,16,128]{2,1,0:T(8,128)(2,1)} %get-tuple-element.12.flat_any, bf16[2,45,4,641]{3,2,1,0:T(4,128)(2,1)} %get-tuple-element.13.lg_any), custom_call_target="tpu_custom_call" | custom-call | tf_op jit(solution)/shard_map/unpack/pallas_call | solution.py:719

commit v3 on v2

--- a/solution.py
+++ b/solution.py
@@ -120,7 +120,6 @@
     wo_any,
     target_any,
     lg,
-    flat_any,
     flat,
     latent,
     seeds,
@@ -166,7 +165,6 @@
     send_sems,
     recv_sems,
     load_sems,
-    store_sems,
 ):
     at = place()
     me = lax.axis_index("member")
@@ -337,14 +335,6 @@
     ).astype(bf16)
 
     factor = 1.0 / math.sqrt(46080.0)
-    stores = []
-
-    def store(start, count):
-        spot = pl.ds(start, count)
-        copy = pltpu.make_async_copy(flat.at[spot], flat_any.at[spot], store_sems.at[len(stores)])
-        copy.start()
-        stores.append(copy)
-
     def add_tiles(dst, dst_at, parts, count, step, scale=None):
         def body(i, carry):
             total = None
@@ -447,9 +437,7 @@
 
         def share(step):
             region = flat.at[pl.ds(block(step, 0), sa)]
-            copy = copies.send(region, region, sibling)
-            store(block(step, 0), sa)
-            return copy
+            return copies.send(region, region, sibling)
 
         from_before = pass_on(0, 0, onward)
         from_after = pass_on(0, 1, backward)
@@ -471,16 +459,15 @@
         far_after.wait_recv()
         last.append(share(2))
         yield
-        for step, copy in zip((0, 3, 1, 2), last):
+        for copy in last:
             copy.wait_recv()
-            store(block(step, 0) + (1 - 2 * core) * size, sa)
         yield
 
     one = [reduced(0, p) for p in range(3)]
     two = [reduced(1, p) for p in range(3)]
 
-    def advance(wave):
-        for part in wave:
+    def advance(*parts):
+        for part in parts:
             next(part)
 
     def put_columns(value, off, units, count):
@@ -495,27 +482,32 @@
 
     value = dot(hid_t[0:656], pg[...])
     put_columns(value, OFF_EXPAND, UNITS, 10)
+    advance(one[0])
     tail = pltpu.roll(value[:, 1280:1408], 4, 1)
     value = dot(mg[...].T[0:656], act[...])
     put_columns(value, OFF_REDUCE, UNITS, 10)
+    advance(one[1], one[0])
     tail = tail + pltpu.roll(value[:, 1280:1408], 6, 1)
     value = dot(fg[...].T[0:OUTC], mix[...])
     put_columns(value, OFF_DECODE, U_DECODE, 5)
     last_lane = jnp.concatenate([value[:, 640:768], jnp.zeros((656 - OUTC, 128), f32)], axis=0)
     tail = tail + pltpu.roll(last_lane, 8, 1)
-    advance(one)
+    advance(one[2], one[1])
 
     hidden_grad = mg[:, 0:CH].astype(f32) + dot_nt(pg[:, 0:HID], we[...])
     hg[:, 0:CH] = hidden_grad.astype(bf16)
+    advance(one[2])
     hg_t = hg[...].T[0:656]
     for c in range(5):
         value = dot(hg_t, spread[:, 512 * c : 512 * c + 512])
         put_columns(value, OFF_DISCO + 4 * c * UNITS, UNITS, 4)
         if c == 1:
-            advance(one)
+            advance(two[0], one[0])
+        if c == 3:
+            advance(two[1], two[0], one[1])
     tail = tail + dot(hg_t, spread[:, 2560:2688])
     put_columns(tail, OFF_TAIL, UNITS, 1)
-    advance(two)
+    advance(two[2], two[1], one[2])
 
     for m in range(2):
         rows = slice(m * HALF, m * HALF + HALF)
@@ -526,17 +518,16 @@
             if k:
                 piece = pltpu.roll(piece, 768 - k, 1)
             sgs[k * HALF : k * HALF + HALF, :] = piece[:, 0:CH].astype(bf16)
-        if m == 0:
-            advance(two)
-            advance(one)
+        advance(two[2] if m == 0 else two[0])
         out = dot(tt[...], sgs[...])
         ob[0, m] = out[240:256]
         ob[1, m] = out[176:192]
         gp[rows, 0:CH] = hg[rows, 0:CH].astype(f32) + out[0:HALF]
+        if m == 0:
+            advance(one[0])
     to_left = copies.send(ob.at[0], back_r.at[0], left)
     to_right = copies.send(ob.at[1], back_r.at[1], right)
-    advance(two)
-    advance(one)
+    advance(one[1], two[1], one[2], two[2], one[0])
     to_left.wait_recv()
     to_right.wait_recv()
     low = iota((16, CH), 0)
@@ -551,77 +542,60 @@
         gp[spot, 0:CH] = gp[spot, 0:CH] + before
         total = gp[base : base + HALF, 0:CH]
         lg[m] = total[0:POINTS].reshape(45, 4, CH).astype(bf16)
-    advance(two)
-    for _ in range(7):
-        advance(one)
-        advance(two)
-    for copy in stores:
-        copy.wait()
+    advance(one[1], one[2])
+    for _ in range(6):
+        advance(*two)
+        advance(*one)
+    advance(*two)
+    advance(*two)
     copies.finish()
 
 
 def unpack_kernel(
-    flat_any,
-    lg_any,
+    flat,
+    lg,
     disco_any,
     expand_any,
     reduce_any,
     decode_any,
     lg_out,
-    flat,
     disco,
     expand,
     reduce,
     decode,
-    lg,
-    in_sems,
     out_sems,
 ):
-    pieces = [(OFF_TAIL, UNITS), (OFF_EXPAND, 410), (OFF_REDUCE, 410), (OFF_DECODE, 90)]
-    pieces += [(OFF_DISCO + 205 * q, 205) for q in range(4)]
-    loads = []
-    for i, (start, count) in enumerate(pieces):
-        spot = pl.ds(start, count)
-        loads.append(pltpu.make_async_copy(flat_any.at[spot], flat.at[spot], in_sems.at[i]))
-        loads[-1].start()
-    loads.append(pltpu.make_async_copy(lg_any, lg, in_sems.at[8]))
-    loads[-1].start()
     stores = []
 
     def store(src, dst):
         stores.append(pltpu.make_async_copy(src, dst, out_sems.at[len(stores)]))
         stores[-1].start()
 
+    store(lg, lg_out)
+
     def column(start, units):
         return flat[start : start + units].reshape(units * 16, 128)
 
-    loads[0].wait()
     tail = column(OFF_TAIL, UNITS)
     wide_tail = tail.astype(f32)
-    loads[1].wait()
     for j in range(10):
         expand[:, 128 * j : 128 * j + 128] = column(OFF_EXPAND + j * UNITS, UNITS)[0:CH]
     expand[:, 1280:HID] = pltpu.roll(wide_tail, 124, 1)[0:CH, 0:2].astype(bf16)
     store(expand, expand_any)
-    loads[2].wait()
     for j in range(10):
         reduce[:, 128 * j : 128 * j + 128] = column(OFF_REDUCE + j * UNITS, UNITS)[0:CH]
     reduce[:, 1280:HID] = pltpu.roll(wide_tail, 122, 1)[0:CH, 0:2].astype(bf16)
     store(reduce, reduce_any)
-    loads[3].wait()
     for j in range(5):
         decode[:, 128 * j : 128 * j + 128] = column(OFF_DECODE + j * U_DECODE, U_DECODE)
     decode[:, 640:CH] = pltpu.roll(wide_tail, 120, 1)[0:OUTC, 0:1].astype(bf16)
     store(decode, decode_any)
     disco[:, 2560:WIDE] = tail[0:CH, 0:4]
     for q in range(4):
-        loads[4 + q].wait()
         for j in range(5 * q, 5 * q + 5):
             disco[:, 128 * j : 128 * j + 128] = column(OFF_DISCO + j * UNITS, UNITS)[0:CH]
         spot = slice(640 * q, WIDE if q == 3 else 640 * q + 640)
         store(disco.at[:, spot], disco_any.at[:, spot])
-    loads[8].wait()
-    store(lg, lg_out)
     for copy in stores:
         copy.wait()
 
@@ -643,7 +617,6 @@
     V = pltpu.VMEM
     copies = 180
     scratch = [
-        V((TILES, 16, 128), bf16),
         V((2, 45, 4, CH), bf16),
         pltpu.SMEM((2,), jnp.int32),
         V((64, CH), bf16),
@@ -688,19 +661,18 @@
         pltpu.SemaphoreType.DMA((copies,)),
         pltpu.SemaphoreType.DMA((copies,)),
         pltpu.SemaphoreType.DMA((10,)),
-        pltpu.SemaphoreType.DMA((48,)),
     ]
     lg, flat = pl.pallas_call(
         step_kernel,
         out_shape=(
-            jax.ShapeDtypeStruct((2, 45, 4, CH), bf16),
-            jax.ShapeDtypeStruct((TILES, 16, 128), bf16),
+            V((2, 45, 4, CH), bf16),
+            V((TILES, 16, 128), bf16),
         ),
         in_specs=[hbm] * 10,
-        out_specs=(vm, hbm),
+        out_specs=(vm, vm),
         scratch_shapes=scratch,
         compiler_params=pltpu.CompilerParams(
-            collective_id=0, has_side_effects=True, vmem_limit_bytes=67_000_000
+            collective_id=0, has_side_effects=True, vmem_limit_bytes=58000000
         ),
         name="step",
     )(
@@ -719,12 +691,11 @@
     disco, expand, reduce, decode, lg = pl.pallas_call(
         unpack_kernel,
         out_shape=tuple(jax.ShapeDtypeStruct(shape, bf16) for shape in shapes),
-        in_specs=[hbm, hbm],
+        in_specs=[vm, vm],
         out_specs=(hbm,) * 5,
-        scratch_shapes=[V((TILES, 16, 128), bf16)]
-        + [V(shape, bf16) for shape in shapes]
-        + [pltpu.SemaphoreType.DMA((9,)), pltpu.SemaphoreType.DMA((8,))],
-        compiler_params=pltpu.CompilerParams(vmem_limit_bytes=67_000_000),
+        scratch_shapes=[V(shape, bf16) for shape in shapes[:4]]
+        + [pltpu.SemaphoreType.DMA((8,))],
+        compiler_params=pltpu.CompilerParams(vmem_limit_bytes=24_000_000),
         name="unpack",
     )(flat, lg)
     return (lg.transpose(0, 2, 1, 3), disco.T, expand, reduce.T, decode.T)

time: 91.8 us -> 90.4 us (0.985)
  Pallas kernels: 90.9 us -> 89.4 us
    pallas_call x1, Pallas kernels: 5.39 us -> 3.52 us  [per_device(): pl.pallas_call(unpack_kernel, out_shape=tuple((jax.ShapeDtypeStruct(shape...]
where the time goes in v3:
time: 90.4 us; the launch traced here: 90.3 us
  Pallas kernels  89.4 us (99%)
    pallas_call x1, Pallas kernels, per_device(): pl.pallas_call(step_kernel, out_shape=(V((2, 45, 4, CH), bf16), V((TILES,...  85.9 us
    pallas_call x1, Pallas kernels, per_device(): pl.pallas_call(unpack_kernel, out_shape=tuple((jax.ShapeDtypeStruct(shape...  3.52 us

profile of v3, /device:TPU:1, one launch (start us, length us, event | category | flops | bytes accessed | tf_op | source)
XLA Modules:
  0.0 90.3 jit_solution(15308764150541447052)
XLA Ops:
  0.6 85.9 %step.1 = (bf16[2,45,4,641]{3,2,1,0:T(4,128)(2,1)S(1)}, bf16[1824,16,128]{2,1,0:T(8,128)(2,1)S(1)}) custom-call(bf16[2,45,4,641]{3,2,1,0:T(4,128)(2,1)} %bitcast.12, s32[2]{0:T(128)} %seeds_any.1, bf16[64,641]{1,0:T(8,128)(2,1)} %table_any.1, s32[4]{0:T(128)} %bands_any.1, bf16[7,7,4,16]{3,2,1,0:T(4,128)(2,1)} %bitcast.15, bf16[641,2564]{1,0:T(8,128)(2,1)} %bitcast.10, ...), custom_call_target="tpu_custom_call" | custom-call | tf_op jit(solution)/shard_map/step/pallas_call | solution.py:665
  86.6 3.5 %unpack.1 = (bf16[641,2564]{1,0:T(8,128)(2,1)}, bf16[641,1282]{1,0:T(8,128)(2,1)}, bf16[641,1282]{1,0:T(8,128)(2,1)}, bf16[288,641]{1,0:T(8,128)(2,1)}, bf16[2,45,4,641]{3,2,1,0:T(4,128)(2,1)}) custom-call(bf16[1824,16,128]{2,1,0:T(8,128)(2,1)S(1)} %get-tuple-element.12.flat, bf16[2,45,4,641]{3,2,1,0:T(4,128)(2,1)S(1)} %get-tuple-element.13.lg), custom_call_target="tpu_custom_call" | custom-call | tf_op jit(solution)/shard_map/unpack/pallas_call | solution.py:691

commit v4 on v3

--- a/solution.py
+++ b/solution.py
@@ -224,10 +224,6 @@
         halo_s[0, m] = jnp.where(low4, 0.0, first).astype(bf16)
         halo_s[1, m] = jnp.where(low4, 0.0, final).astype(bf16)
 
-    pl.semaphore_wait(barrier, len(greet))
-    from_right = copies.send(halo_s.at[0], halo_r.at[0], left)
-    from_left = copies.send(halo_s.at[1], halo_r.at[1], right)
-
     line = iota((8, 16), 0) & 3
     chosen = jnp.where(line == 0, bands[0], jnp.where(line == 1, bands[1], bands[2]))
     chosen = jnp.where(line == 3, bands[3], chosen)
@@ -243,7 +239,7 @@
     spot = (4 * (pair - 7 * a) + a + (256 - 15)) & 255
     hit = iota((196, 256), 1) == spot
     sub = iota((8, 256), 0)
-    for k in range(4):
+    def stencil_matrix(k):
         place_k = jnp.where(hit & ((index & 3) == k), 1.0, 0.0).astype(bf16)
         first = pltpu.roll(dot(taps, place_k), 0, 1, stride=1, stride_axis=0)
         lines = [first if i == 0 else pltpu.roll(first, 8 * i, 1) for i in range(23)]
@@ -251,12 +247,14 @@
         lines.append(jnp.zeros((8, 256), f32))
         band = jnp.concatenate(lines, axis=0).astype(bf16)
         tk[k] = band
-        tt[:, k * HALF : k * HALF + HALF] = band.T
-    tp[0:176] = target[0:44].astype(f32).reshape(176, OUTC)
-    tp[176:184] = jnp.concatenate(
-        [target[44].astype(f32), jnp.zeros((4, OUTC), f32)], axis=0
-    )
-    tp[184:192] = jnp.zeros((8, OUTC), f32)
+
+    stencil_matrix(0)
+    stencil_matrix(1)
+    pl.semaphore_wait(barrier, len(greet))
+    from_right = copies.send(halo_s.at[0], halo_r.at[0], left)
+    from_left = copies.send(halo_s.at[1], halo_r.at[1], right)
+    stencil_matrix(2)
+    stencil_matrix(3)
 
     from_right.wait_recv()
     from_left.wait_recv()
@@ -283,12 +281,9 @@
     hid[:, 0:CH] = (hs[:, 0:CH].astype(f32) + conv).astype(bf16)
     pre = dot(hid[:, 0:CH], we[...])
     inner = math.sqrt(2.0 / math.pi)
-    square = pre * pre
-    t = jnp.tanh(inner * (pre + 0.044715 * (square * pre)))
+    gp[...] = pre
+    t = jnp.tanh(inner * (pre + 0.044715 * (pre * pre * pre)))
     act[:, 0:HID] = (0.5 * pre * (1.0 + t)).astype(bf16)
-    gp[...] = 0.5 * (1.0 + t) + (0.5 * inner) * pre * (1.0 - t * t) * (
-        1.0 + (3.0 * 0.044715) * square
-    )
     mix[:, 0:CH] = (hid[:, 0:CH].astype(f32) + dot_nt(act[:, 0:HID], wr[...])).astype(bf16)
     fields = dot_nt(mix[:, 0:CH], wo[...])
     for p in range(8):
@@ -302,6 +297,19 @@
         there.append(copies.send(fs.at[peer], fr.at[me], (peer, lon)))
     fr[me] = fs[me]
     hid_t[...] = hid[...].T
+    pre = gp[...]
+    square = pre * pre
+    t = jnp.tanh(inner * (pre + 0.044715 * (square * pre)))
+    gp[...] = 0.5 * (1.0 + t) + (0.5 * inner) * pre * (1.0 - t * t) * (
+        1.0 + (3.0 * 0.044715) * square
+    )
+    for k in range(4):
+        tt[:, k * HALF : k * HALF + HALF] = tk[k].T
+    tp[0:176] = target[0:44].astype(f32).reshape(176, OUTC)
+    tp[176:184] = jnp.concatenate(
+        [target[44].astype(f32), jnp.zeros((4, OUTC), f32)], axis=0
+    )
+    tp[184:192] = jnp.zeros((8, OUTC), f32)
 
     for copy in there:
         copy.wait_recv()

time: 90.4 us -> 90.3 us (level)
  no operation moved by 1% of the time
where the time goes in v4:
time: 90.3 us; the launch traced here: 90.2 us
  Pallas kernels  89.4 us (99%)
    pallas_call x1, Pallas kernels, per_device(): pl.pallas_call(step_kernel, out_shape=(V((2, 45, 4, CH), bf16), V((TILES,...  85.9 us
    pallas_call x1, Pallas kernels, per_device(): pl.pallas_call(unpack_kernel, out_shape=tuple((jax.ShapeDtypeStruct(shape...  3.52 us

profile of v4, /device:TPU:1, one launch (start us, length us, event | category | flops | bytes accessed | tf_op | source)
XLA Modules:
  0.0 90.2 jit_solution(10003580771661227531)
XLA Ops:
  0.6 85.9 %step.1 = (bf16[2,45,4,641]{3,2,1,0:T(4,128)(2,1)S(1)}, bf16[1824,16,128]{2,1,0:T(8,128)(2,1)S(1)}) custom-call(bf16[2,45,4,641]{3,2,1,0:T(4,128)(2,1)} %bitcast.12, s32[2]{0:T(128)} %seeds_any.1, bf16[64,641]{1,0:T(8,128)(2,1)} %table_any.1, s32[4]{0:T(128)} %bands_any.1, bf16[7,7,4,16]{3,2,1,0:T(4,128)(2,1)} %bitcast.15, bf16[641,2564]{1,0:T(8,128)(2,1)} %bitcast.10, ...), custom_call_target="tpu_custom_call" | custom-call | tf_op jit(solution)/shard_map/step/pallas_call | solution.py:673
  86.5 3.5 %unpack.1 = (bf16[641,2564]{1,0:T(8,128)(2,1)}, bf16[641,1282]{1,0:T(8,128)(2,1)}, bf16[641,1282]{1,0:T(8,128)(2,1)}, bf16[288,641]{1,0:T(8,128)(2,1)}, bf16[2,45,4,641]{3,2,1,0:T(4,128)(2,1)}) custom-call(bf16[1824,16,128]{2,1,0:T(8,128)(2,1)S(1)} %get-tuple-element.12.flat, bf16[2,45,4,641]{3,2,1,0:T(4,128)(2,1)S(1)} %get-tuple-element.13.lg), custom_call_target="tpu_custom_call" | custom-call | tf_op jit(solution)/shard_map/unpack/pallas_call | solution.py:699

commit v5 on v4

--- a/solution.py
+++ b/solution.py
@@ -62,6 +62,24 @@
 
 def flat_tiles(value):
     return value.astype(bf16).reshape(value.shape[0] // 16, 16, 128)
+
+
+def put_block(ref, p, block):
+    for i in range(3):
+        for j in range(2):
+            ref[p, 2 * i + j] = block[16 * i : 16 * i + 16, 128 * j : 128 * j + 128].astype(bf16)
+    ends = [block[16 * i : 16 * i + 16, 256:OUTC] for i in range(3)]
+    ref[p, 6] = jnp.concatenate(ends + [jnp.zeros((16, 32), f32)], axis=1).astype(bf16)
+
+
+def take_block(ref, p):
+    columns = [
+        jnp.concatenate([ref[p, 2 * i + j].astype(f32) for i in range(3)], axis=0)
+        for j in range(2)
+    ]
+    ends = ref[p, 6].astype(f32)
+    parts = [ends if i == 0 else pltpu.roll(ends, 128 - 32 * i, 1) for i in range(3)]
+    return columns + [jnp.concatenate(parts, axis=0)[:, 0:32]]
 
 
 class Copies:
@@ -290,7 +308,7 @@
         block = jnp.concatenate(
             [fields[24 * p : 24 * p + 24], fields[HALF + 24 * p : HALF + 24 * p + 24]], axis=0
         )
-        fs[p] = block.astype(bf16)
+        put_block(fs, p, block)
     there = []
     for d in range(1, 8):
         peer = lax.rem(me + d, 8)
@@ -314,9 +332,10 @@
     for copy in there:
         copy.wait_recv()
     for p in range(8):
-        block = fr[p].astype(f32)
-        fv[2 * p] = block[0:24]
-        fv[2 * p + 1] = block[24:48]
+        for lo, piece in zip((0, 128, 256), take_block(fr, p)):
+            wide_to = slice(lo, min(lo + 128, OUTC))
+            fv[2 * p, :, wide_to] = piece[0:24]
+            fv[2 * p + 1, :, wide_to] = piece[24:48]
 
     def slopes(i, carry):
         start = pl.multiple_of(i * 8, 8)
@@ -329,7 +348,7 @@
 
     lax.fori_loop(0, 3, slopes, 0)
     for p in range(8):
-        gs[p] = jnp.concatenate([og[2 * p], og[2 * p + 1]], axis=0).astype(bf16)
+        put_block(gs, p, jnp.concatenate([og[2 * p], og[2 * p + 1]], axis=0))
     back = []
     for d in range(1, 8):
         peer = lax.rem(me + d, 8)
@@ -337,10 +356,10 @@
     gr[me] = gs[me]
     for copy in back:
         copy.wait_recv()
-    blocks = [gr[p].astype(f32) for p in range(8)]
-    fg[:, 0:OUTC] = jnp.concatenate(
-        [b[0:24] for b in blocks] + [b[24:48] for b in blocks], axis=0
-    ).astype(bf16)
+    blocks = [take_block(gr, p) for p in range(8)]
+    for q, lo in enumerate((0, 128, 256)):
+        pieces = [b[q][0:24] for b in blocks] + [b[q][24:48] for b in blocks]
+        fg[:, lo : min(lo + 128, OUTC)] = jnp.concatenate(pieces, axis=0).astype(bf16)
 
     factor = 1.0 / math.sqrt(46080.0)
     def add_tiles(dst, dst_at, parts, count, step, scale=None):
@@ -647,12 +666,12 @@
         V((ROWS, 768), bf16),
         V((2, 2, 16, 768), bf16),
         V((2, 2, 16, 768), bf16),
-        V((8, 48, OUTC), bf16),
-        V((8, 48, OUTC), bf16),
+        V((8, 7, 16, 128), bf16),
+        V((8, 7, 16, 128), bf16),
         V((16, 24, OUTC), f32),
         V((16, 24, OUTC), f32),
-        V((8, 48, OUTC), bf16),
-        V((8, 48, OUTC), bf16),
+        V((8, 7, 16, 128), bf16),
+        V((8, 7, 16, 128), bf16),
         V((HALF, OUTC), f32),
         V((ROWS, 384), bf16),
         V((ROWS, 768), bf16),

time: 90.3 us -> 89 us (0.986)
  Pallas kernels: 89.4 us -> 88 us
    pallas_call x1, Pallas kernels: 85.9 us -> 84.5 us  [per_device(): pl.pallas_call(step_kernel, out_shape=(V((2, 45, 4, CH), bf16), V((TILES,...]
where the time goes in v5:
time: 89 us; the launch traced here: 88.8 us
  Pallas kernels  88 us (99%)
    pallas_call x1, Pallas kernels, per_device(): pl.pallas_call(step_kernel, out_shape=(V((2, 45, 4, CH), bf16), V((TILES,...  84.5 us
    pallas_call x1, Pallas kernels, per_device(): pl.pallas_call(unpack_kernel, out_shape=tuple((jax.ShapeDtypeStruct(shape...  3.52 us

profile of v5, /device:TPU:1, one launch (start us, length us, event | category | flops | bytes accessed | tf_op | source)
XLA Modules:
  0.0 88.8 jit_solution(16613888888322550242)
XLA Ops:
  0.6 84.5 %step.1 = (bf16[2,45,4,641]{3,2,1,0:T(4,128)(2,1)S(1)}, bf16[1824,16,128]{2,1,0:T(8,128)(2,1)S(1)}) custom-call(bf16[2,45,4,641]{3,2,1,0:T(4,128)(2,1)} %bitcast.12, s32[2]{0:T(128)} %seeds_any.1, bf16[64,641]{1,0:T(8,128)(2,1)} %table_any.1, s32[4]{0:T(128)} %bands_any.1, bf16[7,7,4,16]{3,2,1,0:T(4,128)(2,1)} %bitcast.15, bf16[641,2564]{1,0:T(8,128)(2,1)} %bitcast.10, ...), custom_call_target="tpu_custom_call" | custom-call | tf_op jit(solution)/shard_map/step/pallas_call | solution.py:692
  85.1 3.5 %unpack.1 = (bf16[641,2564]{1,0:T(8,128)(2,1)}, bf16[641,1282]{1,0:T(8,128)(2,1)}, bf16[641,1282]{1,0:T(8,128)(2,1)}, bf16[288,641]{1,0:T(8,128)(2,1)}, bf16[2,45,4,641]{3,2,1,0:T(4,128)(2,1)}) custom-call(bf16[1824,16,128]{2,1,0:T(8,128)(2,1)S(1)} %get-tuple-element.12.flat, bf16[2,45,4,641]{3,2,1,0:T(4,128)(2,1)S(1)} %get-tuple-element.13.lg), custom_call_target="tpu_custom_call" | custom-call | tf_op jit(solution)/shard_map/unpack/pallas_call | solution.py:718
